TPU v7x, 128 devices: a whole 4x4x4 slice. The times are simulated.
128 devices in a mesh: doc: 8 (over x_lo, z), term: 16 (over y, x_hi, core).
Axes of the slice: x: 4 (x_hi: 2, x_lo: 2; x = x_hi * 2 + x_lo), y: 4, z: 4, core: 2. Of those that a mesh axis runs over, the one named last changes fastest.
Arguments:
- tiles: bfloat16 [8, 16, 8, 512, 512], P('doc', 'term'), may hold values from 0.0009994507 to 1
- tile_rows: int32 [8, 16, 8], P('doc', 'term'), may hold values from 0 to 31, as said below
- tile_cols: int32 [8, 16, 8], P('doc', 'term'), may hold values from 0 to 63
- counts: int32 [8, 16], P('doc', 'term'), may hold values from 2 to 8, as said below
- start_block: float32 [16, 524288], P(None, 'term'), may hold values from -6 to 6
Outputs:
- left_block: float32 [16, 131072], P(None, ('doc', 'term'))
- right_block: float32 [16, 524288], P(None, ('term', 'doc'))
- coefficients: float32 [5, 16, 16], replicated
Inputs may be any that keep to these rules, and one draw needn't show every extreme that they name: On each device the pairs (tile_rows, tile_cols) of its 8 slots are distinct. `counts`: some device uses all 8 slots.
All inputs are finite; a program needn't handle non-finite values.
Results may differ from a plain program's by a relative error of at most 0.0031.
Values sent between devices are 32-bit elements; how exact they have to be, the bound alone decides.
A program may use at most 64 MiB of HBM per device.

v0:
```python
import functools

import jax
import jax.numpy as jnp
from jax import lax
from jax.sharding import Mesh
from jax.sharding import PartitionSpec as P

TERM_TILES = 64
DOC_TILES = 32
DOC = ("doc_0", "doc_1")
TERM = ("term_0", "term_1", "term_2")
DOC_TERM = ("doc_0", "doc_1", "term_0", "term_1", "term_2")
TERM_DOC = ("term_0", "term_1", "term_2", "doc_0", "doc_1")


def sent_to_all(shard, axis):
    peers = lax.axis_size(axis)
    return lax.all_to_all(
        jnp.broadcast_to(shard[None], (peers, *shard.shape)), axis, 0, 0, tiled=True
    )


def of_everyone(shard, axis):
    return sent_to_all(shard, axis).sum(axis=0)


def by_axis(shard, axes):
    return functools.reduce(lax.psum, axes, shard)


def cut_along(shard, dim, peers):
    lengths = shard.shape
    pieces = shard.reshape(*lengths[:dim], peers, lengths[dim] // peers, *lengths[dim + 1 :])
    return jnp.moveaxis(pieces, dim, 0)


def sent_and_summed(shard, axis, dim):
    pieces = cut_along(shard, dim, lax.axis_size(axis))
    arrived = lax.all_to_all(pieces, axis, split_axis=0, concat_axis=0, tiled=True)
    return arrived.sum(axis=0)


def in_order(pieces, dim):
    pieces = jnp.moveaxis(pieces, 0, dim)
    lengths = pieces.shape
    return pieces.reshape(*lengths[:dim], lengths[dim] * lengths[dim + 1], *lengths[dim + 2 :])


def gathered_copies(shard, axis, dim):
    pieces = sent_to_all(shard, axis)
    return in_order(pieces, dim)


def orthonormal(vectors, earlier, total_rows, summed):
    highest = lax.Precision.HIGHEST
    if earlier is None:
        gram_matrix = summed(jnp.dot(vectors, vectors.T, precision=highest) / total_rows)
        factor = jnp.linalg.cholesky(gram_matrix)
        return (jax.scipy.linalg.solve_triangular(factor, vectors, lower=True), factor, None)
    projection = summed(jnp.dot(vectors, earlier.T, precision=highest) / total_rows)
    vectors = vectors - jnp.dot(projection, earlier, precision=highest)
    gram_matrix = summed(jnp.dot(vectors, vectors.T, precision=highest) / total_rows)
    factor = jnp.linalg.cholesky(gram_matrix)
    return (jax.scipy.linalg.solve_triangular(factor, vectors, lower=True), factor, projection)


def on_device(tiles, tile_rows, tile_cols, counts, start_block):
    highest = lax.Precision.HIGHEST
    local_tiles = tiles[0, 0]
    slot_rows = tile_rows[0, 0]
    slot_cols = tile_cols[0, 0]
    in_use = counts[0, 0]
    slot_count = local_tiles.shape[0]
    tile_edge = local_tiles.shape[1]
    block_cols = start_block.shape[0]
    doc_groups = lax.axis_size(DOC)
    term_groups = lax.axis_size(TERM)
    row_count = DOC_TILES * tile_edge
    col_count = TERM_TILES * tile_edge
    n_docs = row_count * doc_groups
    n_terms = col_count * term_groups
    active = (jnp.arange(slot_count) < in_use).astype(jnp.float32)
    row_onehot = (slot_rows[:, None] == jnp.arange(DOC_TILES)[None, :]).astype(jnp.float32)
    col_onehot = (slot_cols[:, None] == jnp.arange(TERM_TILES)[None, :]).astype(jnp.float32)
    row_live = row_onehot * active[:, None]
    col_live = col_onehot * active[:, None]
    ones_edge = jnp.ones((tile_edge,), jnp.bfloat16)
    row_sums = jnp.einsum("kab,b->ka", local_tiles, ones_edge, preferred_element_type=jnp.float32)
    col_sums = jnp.einsum("kab,a->kb", local_tiles, ones_edge, preferred_element_type=jnp.float32)
    row_part = jnp.einsum("kr,ka->ra", row_live, row_sums, precision=highest).reshape(-1)
    col_part = jnp.einsum("kc,kb->cb", col_live, col_sums, precision=highest).reshape(-1)
    row_scale = lax.rsqrt(of_everyone(row_part, TERM) + 1.0)
    col_scale = lax.rsqrt(of_everyone(col_part, DOC) + 1.0)
    start_gram = of_everyone(jnp.dot(start_block, start_block.T, precision=highest) / n_terms, TERM)
    first_right = jax.scipy.linalg.solve_triangular(
        jnp.linalg.cholesky(start_gram), start_block, lower=True
    )

    def forward(right_block):
        scaled = (
            (right_block * col_scale[None, :])
            .astype(jnp.bfloat16)
            .reshape(block_cols, TERM_TILES, tile_edge)
        )
        pieces = jnp.einsum(
            "kc,bcx->kbx",
            col_onehot.astype(jnp.bfloat16),
            scaled,
            preferred_element_type=jnp.float32,
        ).astype(jnp.bfloat16)
        product = jnp.einsum(
            "kab,kcb->kca", local_tiles, pieces, preferred_element_type=jnp.float32
        )
        return jnp.einsum("kr,kca->cra", row_live, product, precision=highest).reshape(
            block_cols, row_count
        )

    share_rows = row_count // term_groups
    share_cols = col_count // doc_groups
    row_share = lax.dynamic_slice_in_dim(
        row_scale, lax.axis_index(TERM) * share_rows, share_rows, 0
    )
    col_share = lax.dynamic_slice_in_dim(col_scale, lax.axis_index(DOC) * share_cols, share_cols, 0)
    first_share = lax.dynamic_slice_in_dim(
        first_right, lax.axis_index(DOC) * share_cols, share_cols, 1
    )

    def doc_total(partial_value):
        return by_axis(partial_value, DOC_TERM)

    def term_total(partial_value):
        return by_axis(partial_value, DOC_TERM)

    def doc_side(right_block):
        return sent_and_summed(forward(right_block), TERM, 1) * row_share[None, :]

    left_one, factor_one, nothing = orthonormal(doc_side(first_right), None, n_docs, doc_total)
    left_full = gathered_copies(left_one, TERM, 1)
    scaled = (
        (left_full * row_scale[None, :])
        .astype(jnp.bfloat16)
        .reshape(block_cols, DOC_TILES, tile_edge)
    )
    pieces = jnp.einsum(
        "kr,brx->kbx", row_onehot.astype(jnp.bfloat16), scaled, preferred_element_type=jnp.float32
    ).astype(jnp.bfloat16)
    product = jnp.einsum("kab,kca->kcb", local_tiles, pieces, preferred_element_type=jnp.float32)
    right_raw = (
        sent_and_summed(
            jnp.einsum("kc,kxb->xcb", col_live, product, precision=highest).reshape(
                block_cols, col_count
            ),
            DOC,
            1,
        )
        * col_share[None, :]
    )
    right_out, factor_two, projection_one = orthonormal(right_raw, first_share, n_terms, term_total)
    right_full = gathered_copies(right_out, DOC, 1)
    left_out, factor_three, projection_two = orthonormal(
        doc_side(right_full), left_one, n_docs, doc_total
    )
    coefficients = jnp.stack([factor_one, projection_one, factor_two, projection_two, factor_three])
    return (left_out, right_out, coefficients)


def solution(mesh):
    split = Mesh(
        mesh.devices.reshape(2, 4, 4, 2, 2), ("doc_0", "doc_1", "term_0", "term_1", "term_2")
    )
    placed = (
        P(DOC, TERM, None, None, None),
        P(DOC, TERM, None),
        P(DOC, TERM, None),
        P(DOC, TERM),
        P(None, TERM),
    )
    return jax.shard_map(
        on_device,
        mesh=split,
        in_specs=placed,
        out_specs=(P(None, DOC_TERM), P(None, TERM_DOC), P()),
        check_vma=False,
    )
```

profile of v0, /device:TPU:1, one launch (start us, length us, event | category | flops | bytes accessed | tf_op | source)
XLA Modules:
  0.0 412.8 jit_solution(10469929191016408922)
XLA Ops:
  5.9 8.4 %all-to-all-start = ((f32[16,1,256]{2,1,0:T(1,128)}), f32[16,1,256]{2,1,0:T(1,128)S(1)}, u32[]{:S(2)}, u32[]{:S(2)}) async-start(f32[16,1,256]{2,1,0:T(1,128)} %reshape.100), calls=%async_computation | async-start | bytes 32768 | tf_op jit(solution)/shard_map/all_to_all | solution.py:19
  37.3 5.8 %all-to-all-done.1 = f32[8,1,32768]{2,1,0:T(1,128)S(1)} async-done(((f32[8,1,32768]{2,1,0:T(1,128)}), f32[8,1,32768]{2,1,0:T(1,128)S(1)}, u32[]{:S(2)}, u32[]{:S(2)}) %all-to-all-start.1) | async-done | bytes 1048608 | tf_op jit(solution)/shard_map/all_to_all | solution.py:19
  72.6 16.5 %all-to-all-done.2 = f32[16,16,1024]{2,1,0:T(8,128)} async-done(((f32[16,16,1024]{2,1,0:T(8,128)}), f32[16,16,1024]{2,1,0:T(8,128)}, u32[]{:S(2)}, u32[]{:S(2)}) %all-to-all-start.2) | async-done | bytes 1048608 | tf_op jit(solution)/shard_map/all_to_all | solution.py:40
  94.5 7.3 %psum.176 = f32[16,16]{1,0:T(8,128)S(1)} all-reduce(f32[16,16]{1,0:T(8,128)S(1)} %psum.175), channel_id=1, replica_groups=mesh['doc_0'=2,'doc_1'=4,'term_0'=4,'term_1'=2,'term_2'=2] {'doc_1'}, use_global_device_ids=true, to_apply=%region_7.9 | all-reduce | flops 256 | bytes 2048 | tf_op jit(solution)/shard_map/psum | solution.py:29
  101.8 6.7 %psum.177 = f32[16,16]{1,0:T(8,128)S(1)} all-reduce(f32[16,16]{1,0:T(8,128)S(1)} %psum.176), channel_id=1, replica_groups=mesh['doc_0'=2,'doc_1'=4,'term_0'=4,'term_1'=2,'term_2'=2] {'term_0'}, use_global_device_ids=true, to_apply=%region_8.10 | all-reduce | flops 256 | bytes 2048 | tf_op jit(solution)/shard_map/psum | solution.py:29
  113.8 9.4 %psum.179 = f32[16,16]{1,0:T(8,128)S(1)} all-reduce(f32[16,16]{1,0:T(8,128)S(1)} %psum.178), channel_id=1, replica_groups=mesh['doc_0'=2,'doc_1'=4,'term_0'=4,'term_1'=2,'term_2'=2] {'term_2'}, use_global_device_ids=true, to_apply=%region_10.12 | all-reduce | flops 256 | bytes 2048 | tf_op jit(solution)/shard_map/psum | solution.py:29
  133.3 17.2 %all-to-all-done.4 = f32[16,16,1024]{2,1,0:T(8,128)S(1)} async-done(((f32[16,16,1024]{2,1,0:T(8,128)}), f32[16,16,1024]{2,1,0:T(8,128)S(1)}, u32[]{:S(2)}, u32[]{:S(2)}) %all-to-all-start.4) | async-done | bytes 1048608 | tf_op jit(solution)/shard_map/all_to_all | solution.py:19
  171.1 26.2 %all-to-all-done.5 = f32[8,16,4096]{2,1,0:T(8,128)} async-done(((f32[8,16,4096]{2,1,0:T(8,128)}), f32[8,16,4096]{2,1,0:T(8,128)}, u32[]{:S(2)}, u32[]{:S(2)}) %all-to-all-start.5) | async-done | bytes 2097184 | tf_op jit(solution)/shard_map/all_to_all | solution.py:40
  204.3 7.3 %psum.181 = f32[16,16]{1,0:T(8,128)S(1)} all-reduce(f32[16,16]{1,0:T(8,128)S(1)} %psum.180), channel_id=1, replica_groups=mesh['doc_0'=2,'doc_1'=4,'term_0'=4,'term_1'=2,'term_2'=2] {'doc_1'}, use_global_device_ids=true, to_apply=%region_13.16 | all-reduce | flops 256 | bytes 2048 | tf_op jit(solution)/shard_map/psum | solution.py:29
  211.5 6.7 %psum.182 = f32[16,16]{1,0:T(8,128)S(1)} all-reduce(f32[16,16]{1,0:T(8,128)S(1)} %psum.181), channel_id=1, replica_groups=mesh['doc_0'=2,'doc_1'=4,'term_0'=4,'term_1'=2,'term_2'=2] {'term_0'}, use_global_device_ids=true, to_apply=%region_14.17 | all-reduce | flops 256 | bytes 2048 | tf_op jit(solution)/shard_map/psum | solution.py:29
  218.2 5.4 %psum.183 = f32[16,16]{1,0:T(8,128)S(1)} all-reduce(f32[16,16]{1,0:T(8,128)S(1)} %psum.182), channel_id=1, replica_groups=mesh['doc_0'=2,'doc_1'=4,'term_0'=4,'term_1'=2,'term_2'=2] {'term_1'}, use_global_device_ids=true, to_apply=%region_15.18 | all-reduce | flops 256 | bytes 2048 | tf_op jit(solution)/shard_map/psum | solution.py:29
  223.5 9.7 %psum.184 = f32[16,16]{1,0:T(8,128)S(1)} all-reduce(f32[16,16]{1,0:T(8,128)S(1)} %psum.183), channel_id=1, replica_groups=mesh['doc_0'=2,'doc_1'=4,'term_0'=4,'term_1'=2,'term_2'=2] {'term_2'}, use_global_device_ids=true, to_apply=%region_16.19 | all-reduce | flops 256 | bytes 2048 | tf_op jit(solution)/shard_map/psum | solution.py:29
  238.8 6.1 %psum.186 = f32[16,16]{1,0:T(8,128)S(1)} all-reduce(f32[16,16]{1,0:T(8,128)S(1)} %psum.185), channel_id=1, replica_groups=mesh['doc_0'=2,'doc_1'=4,'term_0'=4,'term_1'=2,'term_2'=2] {'doc_1'}, use_global_device_ids=true, to_apply=%region_18.21 | all-reduce | flops 256 | bytes 2048 | tf_op jit(solution)/shard_map/psum | solution.py:29
  244.9 7.0 %psum.187 = f32[16,16]{1,0:T(8,128)S(1)} all-reduce(f32[16,16]{1,0:T(8,128)S(1)} %psum.186), channel_id=1, replica_groups=mesh['doc_0'=2,'doc_1'=4,'term_0'=4,'term_1'=2,'term_2'=2] {'term_0'}, use_global_device_ids=true, to_apply=%region_19.22 | all-reduce | flops 256 | bytes 2048 | tf_op jit(solution)/shard_map/psum | solution.py:29
  251.9 5.4 %psum.188 = f32[16,16]{1,0:T(8,128)S(1)} all-reduce(f32[16,16]{1,0:T(8,128)S(1)} %psum.187), channel_id=1, replica_groups=mesh['doc_0'=2,'doc_1'=4,'term_0'=4,'term_1'=2,'term_2'=2] {'term_1'}, use_global_device_ids=true, to_apply=%region_20.23 | all-reduce | flops 256 | bytes 2048 | tf_op jit(solution)/shard_map/psum | solution.py:29
  257.3 8.7 %psum.189 = f32[16,16]{1,0:T(8,128)S(1)} all-reduce(f32[16,16]{1,0:T(8,128)S(1)} %psum.188), channel_id=1, replica_groups=mesh['doc_0'=2,'doc_1'=4,'term_0'=4,'term_1'=2,'term_2'=2] {'term_2'}, use_global_device_ids=true, to_apply=%region_21.24 | all-reduce | flops 256 | bytes 2048 | tf_op jit(solution)/shard_map/psum | solution.py:29
  276.7 25.9 %all-to-all-done.6 = f32[8,16,4096]{2,1,0:T(8,128)} async-done(((f32[8,16,4096]{2,1,0:T(8,128)}), f32[8,16,4096]{2,1,0:T(8,128)}, u32[]{:S(2)}, u32[]{:S(2)}) %all-to-all-start.6) | async-done | bytes 2097184 | tf_op jit(solution)/shard_map/all_to_all | solution.py:19
  325.9 15.9 %all-to-all-done.7 = f32[16,16,1024]{2,1,0:T(8,128)S(1)} async-done(((f32[16,16,1024]{2,1,0:T(8,128)}), f32[16,16,1024]{2,1,0:T(8,128)S(1)}, u32[]{:S(2)}, u32[]{:S(2)}) %all-to-all-start.7) | async-done | bytes 1048608 | tf_op jit(solution)/shard_map/all_to_all | solution.py:40
  345.9 8.0 %psum.191 = f32[16,16]{1,0:T(8,128)S(1)} all-reduce(f32[16,16]{1,0:T(8,128)S(1)} %psum.190), channel_id=1, replica_groups=mesh['doc_0'=2,'doc_1'=4,'term_0'=4,'term_1'=2,'term_2'=2] {'doc_1'}, use_global_device_ids=true, to_apply=%region_24.27 | all-reduce | flops 256 | bytes 2048 | tf_op jit(solution)/shard_map/psum | solution.py:29
  353.9 6.6 %psum.192 = f32[16,16]{1,0:T(8,128)S(1)} all-reduce(f32[16,16]{1,0:T(8,128)S(1)} %psum.191), channel_id=1, replica_groups=mesh['doc_0'=2,'doc_1'=4,'term_0'=4,'term_1'=2,'term_2'=2] {'term_0'}, use_global_device_ids=true, to_apply=%region_25.28 | all-reduce | flops 256 | bytes 2048 | tf_op jit(solution)/shard_map/psum | solution.py:29
  365.8 9.2 %psum.194 = f32[16,16]{1,0:T(8,128)S(1)} all-reduce(f32[16,16]{1,0:T(8,128)S(1)} %psum.193), channel_id=1, replica_groups=mesh['doc_0'=2,'doc_1'=4,'term_0'=4,'term_1'=2,'term_2'=2] {'term_2'}, use_global_device_ids=true, to_apply=%region_27.30 | all-reduce | flops 256 | bytes 2048 | tf_op jit(solution)/shard_map/psum | solution.py:29
  379.2 6.1 %psum.196 = f32[16,16]{1,0:T(8,128)S(1)} all-reduce(f32[16,16]{1,0:T(8,128)S(1)} %psum.195), channel_id=1, replica_groups=mesh['doc_0'=2,'doc_1'=4,'term_0'=4,'term_1'=2,'term_2'=2] {'doc_1'}, use_global_device_ids=true, to_apply=%region_29.32 | all-reduce | flops 256 | bytes 2048 | tf_op jit(solution)/shard_map/psum | solution.py:29
  385.3 7.1 %psum.197 = f32[16,16]{1,0:T(8,128)S(1)} all-reduce(f32[16,16]{1,0:T(8,128)S(1)} %psum.196), channel_id=1, replica_groups=mesh['doc_0'=2,'doc_1'=4,'term_0'=4,'term_1'=2,'term_2'=2] {'term_0'}, use_global_device_ids=true, to_apply=%region_30.33 | all-reduce | flops 256 | bytes 2048 | tf_op jit(solution)/shard_map/psum | solution.py:29
  397.7 8.8 %psum.199 = f32[16,16]{1,0:T(8,128)S(1)} all-reduce(f32[16,16]{1,0:T(8,128)S(1)} %psum.198), channel_id=1, replica_groups=mesh['doc_0'=2,'doc_1'=4,'term_0'=4,'term_1'=2,'term_2'=2] {'term_2'}, use_global_device_ids=true, to_apply=%region_32.35 | all-reduce | flops 256 | bytes 2048 | tf_op jit(solution)/shard_map/psum | solution.py:29
  (145 shorter events, 170.0 us)
Async XLA Ops:
  0.6 1.6 copy-start
  5.9 15.7 %all-to-all-start = ((f32[16,1,256]{2,1,0:T(1,128)}), f32[16,1,256]{2,1,0:T(1,128)S(1)}, u32[]{:S(2)}, u32[]{:S(2)}) async-start(f32[16,1,256]{2,1,0:T(1,128)} %reshape.100), calls=%async_computation | async-start | bytes 32768 | tf_op jit(solution)/shard_map/all_to_all | solution.py:19
  14.3 3.5 copy-start.10
  17.9 138.7 %copy-start.11 = (f32[8]{0:T(128)}, f32[8]{0:T(128)S(1)}, u32[]{:S(2)}) copy-start(f32[8]{0:T(128)S(1)} %compare_convert_fusion) | copy-start | bytes 100
  23.2 19.9 %all-to-all-start.1 = ((f32[8,1,32768]{2,1,0:T(1,128)}), f32[8,1,32768]{2,1,0:T(1,128)S(1)}, u32[]{:S(2)}, u32[]{:S(2)}) async-start(f32[8,1,32768]{2,1,0:T(1,128)} %broadcast_in_dim.20), calls=%async_computation.1 | async-start | bytes 2097152 | tf_op jit(solution)/shard_map/all_to_all | solution.py:19
  28.1 3.4 copy-start.13
  43.0 1.8 copy-start.2
  44.8 22.0 %all-to-all-start.3 = ((f32[16,1,16384]{2,1,0:T(1,128)}), f32[16,1,16384]{2,1,0:T(1,128)S(1)}, u32[]{:S(2)}, u32[]{:S(2)}) async-start(f32[16,1,16384]{2,1,0:T(1,128)} %broadcast_in_dim.22), calls=%async_computation.3 | async-start | bytes 2097152 | tf_op jit(solution)/shard_map/all_to_all | solution.py:19
  51.8 3.9 copy-start.1
  66.8 22.4 %all-to-all-start.2 = ((f32[16,16,1024]{2,1,0:T(8,128)}), f32[16,16,1024]{2,1,0:T(8,128)}, u32[]{:S(2)}, u32[]{:S(2)}) async-start(f32[16,16,1024]{2,1,0:T(8,128)} %bitcast.123), calls=%async_computation.2 | async-start | bytes 2097152 | tf_op jit(solution)/shard_map/all_to_all | solution.py:40
  124.9 4.6 %copy-start.6 = (f32[16,16]{1,0:T(8,128)}, f32[16,16]{1,0:T(8,128)S(1)}, u32[]{:S(2)}) copy-start(f32[16,16]{1,0:T(8,128)S(1)} %cholesky.85) | copy-start | bytes 3076
  127.7 0.6 copy-start.4
  129.5 21.0 %all-to-all-start.4 = ((f32[16,16,1024]{2,1,0:T(8,128)}), f32[16,16,1024]{2,1,0:T(8,128)S(1)}, u32[]{:S(2)}, u32[]{:S(2)}) async-start(f32[16,16,1024]{2,1,0:T(8,128)} %broadcast_in_dim.23), calls=%async_computation.4 | async-start | bytes 2097152 | tf_op jit(solution)/shard_map/all_to_all | solution.py:19
  166.7 30.6 %all-to-all-start.5 = ((f32[8,16,4096]{2,1,0:T(8,128)}), f32[8,16,4096]{2,1,0:T(8,128)}, u32[]{:S(2)}, u32[]{:S(2)}) async-start(f32[8,16,4096]{2,1,0:T(8,128)} %bitcast.122), calls=%async_computation.5 | async-start | bytes 4194304 | tf_op jit(solution)/shard_map/all_to_all | solution.py:40
  267.6 1.3 copy-start.8
  270.6 1.5 copy-start.3
  272.1 30.5 %all-to-all-start.6 = ((f32[8,16,4096]{2,1,0:T(8,128)}), f32[8,16,4096]{2,1,0:T(8,128)}, u32[]{:S(2)}, u32[]{:S(2)}) async-start(f32[8,16,4096]{2,1,0:T(8,128)} %broadcast_in_dim.24), calls=%async_computation.6 | async-start | bytes 4194304 | tf_op jit(solution)/shard_map/all_to_all | solution.py:19
  311.4 3.4 copy-start.12
  311.4 3.4 copy-start.14
  317.4 7.2 %copy-start.7 = (f32[16,16]{1,0:T(8,128)S(1)}, f32[16,16]{1,0:T(8,128)}, u32[]{:S(2)}) copy-start(f32[16,16]{1,0:T(8,128)} %copy-done.6) | copy-start | bytes 3076
  317.4 7.9 %copy-start.9 = (f32[16,16]{1,0:T(8,128)S(1)}, f32[16,16]{1,0:T(8,128)}, u32[]{:S(2)}) copy-start(f32[16,16]{1,0:T(8,128)} %copy-done.8) | copy-start | bytes 3076
  320.2 21.6 %copy-start.5 = (f32[16,1024]{1,0:T(8,128)S(1)}, f32[16,1024]{1,0:T(8,128)}, u32[]{:S(2)}) copy-start(f32[16,1024]{1,0:T(8,128)} %copy-done.4) | copy-start | bytes 196612
  320.2 21.5 %all-to-all-start.7 = ((f32[16,16,1024]{2,1,0:T(8,128)}), f32[16,16,1024]{2,1,0:T(8,128)S(1)}, u32[]{:S(2)}, u32[]{:S(2)}) async-start(f32[16,16,1024]{2,1,0:T(8,128)} %bitcast.124), calls=%async_computation.7 | async-start | bytes 2097152 | tf_op jit(solution)/shard_map/all_to_all | solution.py:40
  412.2 0.6 copy-start.15
where the time goes:
time: 415 us; the launch traced here: 413 us
  blocking collectives  160 us (39%)
  waiting for transfers between devices  113 us (27%)
  starting transfers between devices  40.4 us (10%)
  local copies, waits for them, and re-layouts  37.4 us (9%)
  matrix products  35.2 us (8%)
  other arithmetic  24.5 us (6%)
    psum x25, blocking collectives, by_axis(): return functools.reduce(lax.psum, axes, shard)  160 us
    all_to_all x3, waiting for transfers between devices, sent_and_summed(): lax.all_to_all(pieces, axis, split_axis=0, concat_axis=0, tiled=True)  58.6 us
    all_to_all x5, waiting for transfers between devices, sent_to_all(): lax.all_to_all(jnp.broadcast_to(shard[None], (peers, *shard.shape)), axis...  54.6 us
    all_to_all x5, starting transfers between devices, sent_to_all(): lax.all_to_all(jnp.broadcast_to(shard[None], (peers, *shard.shape)), axis...  26.6 us
    another operation x6, local copies, waits for them, and re-layouts, cut_along(): shard.reshape(*lengths[:dim], peers, lengths[dim] // peers, *lengths[dim...  16.4 us
    all_to_all x3, starting transfers between devices, sent_and_summed(): lax.all_to_all(pieces, axis, split_axis=0, concat_axis=0, tiled=True)  13.8 us
  transfers between devices with their start and end apart: 8, of which 8 were waited for; matrix products, arithmetic and copies ran while one was open for 7% of the time, Pallas kernels for 0%

commit v1 on v0

v1 whole, which is shorter than its diff:
```python
import functools

import jax
import jax.numpy as jnp
from jax import lax
from jax.experimental import pallas as pl
from jax.experimental.pallas import tpu as pltpu
from jax.sharding import PartitionSpec as P

MESH = pl.DeviceIdType.MESH
F32 = jnp.float32
BF16 = jnp.bfloat16
TILE = 512
BLOCK = 16
SLOTS = 8
LANES = SLOTS * BLOCK
TERM_TILES = 64
DOC_TILES = 32
ND = 8
NT = 16
DX = TILE // ND
TX = TILE // NT
DGROUPS = DOC_TILES * BLOCK // LANES
TGROUPS = TERM_TILES * BLOCK // LANES
N_DOCS = ND * DOC_TILES * TILE
N_TERMS = NT * TERM_TILES * TILE
HIGHEST = lax.Precision.HIGHEST


def dot(a, b, contract, precision=HIGHEST):
    return lax.dot_general(
        a, b, (contract, ((), ())), precision=precision, preferred_element_type=F32
    )


NN = ((1,), (0,))
NTR = ((1,), (1,))
TN = ((0,), (0,))


def halves(x):
    hi = x.astype(BF16)
    lo = (x - hi.astype(F32)).astype(BF16)
    return jnp.concatenate([hi, lo], axis=0)


def by_onehot(x, onehot, contract):
    n = x.shape[0]
    both = dot(halves(x), onehot, contract, None)
    return both[:n] + both[n:]


def iota(shape, dim):
    return lax.broadcasted_iota(jnp.int32, shape, dim)


def roll(x, shift):
    return pltpu.roll(x, shift, 1)


def fold(t):
    same = iota((LANES, LANES), 0) // BLOCK == iota((LANES, LANES), 1) // BLOCK
    t = jnp.where(same, t, 0.0)
    w = t[0:BLOCK]
    for g in range(1, SLOTS):
        w = w + t[g * BLOCK : (g + 1) * BLOCK]
    w = w + roll(w, 64)
    w = w + roll(w, 32)
    return w + roll(w, 16)


def packed(s, r):
    group = iota((8, LANES), 1) // BLOCK
    z = jnp.where(group == 0, s[0:8], s[8:16])
    if r is None:
        return z
    return jnp.where(group < 2, z, jnp.where(group == 2, r[0:8], r[8:16]))


def unpacked(z, first):
    lane = iota((BLOCK, LANES), 1)
    top = z if first == 0 else roll(z, LANES - BLOCK * first)
    low = roll(z, LANES - BLOCK * (first + 1))
    return jnp.where(lane < BLOCK, jnp.concatenate([top, low], axis=0), 0.0)


def spread(m):
    same = iota((LANES, LANES), 0) // BLOCK == iota((LANES, LANES), 1) // BLOCK
    r = m + roll(m, 16)
    r = r + roll(r, 32)
    r = r + roll(r, 64)
    return jnp.where(same, jnp.concatenate([r] * SLOTS, axis=0), 0.0)


def factor(s):
    lane = iota((BLOCK, LANES), 1)
    sub = iota((BLOCK, LANES), 0)
    m = jnp.where(lane < BLOCK, s, jnp.where(lane == sub + BLOCK, 1.0, 0.0))
    for c in range(BLOCK - 1):
        ratio = m[c : c + 1, :] / m[c : c + 1, c : c + 1]
        m = m - jnp.where(sub > c, m[:, c : c + 1], 0.0) * ratio
    diag = jnp.sum(jnp.where(lane == sub, m, 0.0), axis=1, keepdims=True)
    m = m * lax.rsqrt(diag)
    upper = jnp.where((lane < BLOCK) & (lane >= sub), m, 0.0)
    inverse = jnp.where(lane < BLOCK, roll(m, LANES - BLOCK), 0.0)
    return upper, inverse


def transposed(m):
    full = jnp.concatenate([m, jnp.zeros((LANES - BLOCK, LANES), F32)], axis=0)
    return full.T[:BLOCK, :]


def kernel(
    rows_s, cols_s, cnt_s, tiles_h, start_h,
    left_o, right_o, coef_o,
    tiles_v, start_v, st_v, sd_v,
    m1_v, d1_v, cs_v,
    tsend, trecv, dsend, drecv, za, zb,
    slots_v, share_v, e_v, u_v, x_v,
    load_sem, send_sem, recv_sem,
):
    i = lax.axis_index("doc")
    j = lax.axis_index("term")
    bar = pltpu.get_barrier_semaphore()
    for d in range(1, ND):
        pl.semaphore_signal(bar, 1, device_id=(lax.rem(i + d, ND), j), device_id_type=MESH)
    for d in range(1, NT):
        pl.semaphore_signal(bar, 1, device_id=(i, lax.rem(j + d, NT)), device_id_type=MESH)

    def load_start(t, carry):
        columns = pl.ds(pl.multiple_of(t * TILE, TILE), TILE)
        pltpu.make_async_copy(start_h.at[:, columns], start_v.at[t], load_sem.at[SLOTS]).start()
        return carry

    lax.fori_loop(0, TERM_TILES, load_start, 0)
    loads = []
    for k in range(SLOTS):
        load = pltpu.make_async_copy(tiles_h.at[k], tiles_v.at[k], load_sem.at[k])
        load.start()
        loads.append(load)

    pending = []

    def to_terms(n, src_of, dst, size):
        def send(d, carry):
            q = lax.rem(j + d, NT)
            pltpu.make_async_remote_copy(
                src_ref=src_of(q), dst_ref=dst.at[j],
                send_sem=send_sem.at[n], recv_sem=recv_sem.at[n],
                device_id=(i, q), device_id_type=MESH,
            ).start()
            return carry
        lax.fori_loop(1, NT, send, 0)
        pending.append((n, dst.at[pl.ds(0, NT - 1)]))

    def to_docs(n, src_of, dst, size):
        def send(d, carry):
            q = lax.rem(i + d, ND)
            pltpu.make_async_remote_copy(
                src_ref=src_of(q), dst_ref=dst.at[i],
                send_sem=send_sem.at[n], recv_sem=recv_sem.at[n],
                device_id=(q, j), device_id_type=MESH,
            ).start()
            return carry
        lax.fori_loop(1, ND, send, 0)
        pending.append((n, dst.at[pl.ds(0, ND - 1)]))

    def arrived(n, dst, peers):
        part = dst.at[pl.ds(0, peers - 1)]
        pltpu.make_async_copy(part, part, recv_sem.at[n]).wait()

    lane8 = iota((8, LANES), 1)
    sub8 = iota((8, LANES), 0)
    cnt = cnt_s[0]
    row_at = jnp.zeros((8, LANES), jnp.int32)
    my_col = jnp.zeros((8, LANES), jnp.int32)
    col_of = jnp.zeros((8, LANES), jnp.int32)
    for k in range(SLOTS):
        here = lane8 // BLOCK == k
        row_at = jnp.where(here, rows_s[k] * BLOCK, row_at)
        my_col = jnp.where(here, cols_s[k], my_col)
        col_of = jnp.where(sub8 == k, cols_s[k], col_of)
    row_at = jnp.where(lane8 // BLOCK < cnt, row_at, -100000)
    my_col = jnp.where(lane8 // BLOCK < cnt, my_col, -10000)
    col_of = jnp.where(sub8 < cnt, col_of, -10000)
    col_at = my_col * BLOCK
    row_at = (row_at + lane8 % BLOCK).astype(F32)
    col_at = (col_at + lane8 % BLOCK).astype(F32)
    my_col = my_col.astype(F32)
    d1_v[i] = jnp.concatenate([col_of.astype(F32), col_at], axis=0)

    pltpu.make_async_copy(start_v, start_v, load_sem.at[SLOTS]).wait()
    acc = jnp.zeros((2 * LANES, 2 * LANES), F32)
    for ch in range(8):
        both = halves(start_v[ch * 8 : (ch + 1) * 8].reshape(LANES, TILE))
        acc = acc + dot(both, both, NTR, None)
    t = acc[:LANES, :LANES] + acc[:LANES, LANES:] + acc[LANES:, :LANES] + acc[LANES:, LANES:]
    m1_v[j] = jnp.concatenate([packed(fold(t) * (1.0 / N_TERMS), None), row_at], axis=0)

    col_sums = jnp.zeros((16, TILE), F32)
    for k in range(SLOTS):
        loads[k].wait()
        ones = jnp.where(iota((16, TILE), 0) == k, 1.0, 0.0).astype(BF16)
        col_sums = col_sums + dot(ones, tiles_v[k], NN, None)
    cs_v[i] = col_sums[:SLOTS]

    pl.semaphore_wait(bar, ND - 1 + NT - 1)
    to_docs(0, lambda q: d1_v.at[i], d1_v, 0)
    to_docs(1, lambda q: cs_v.at[i], cs_v, 0)
    to_terms(2, lambda q: m1_v.at[j], m1_v, 0)

    lane_slot = iota((TILE, LANES), 1) // BLOCK

    def forward_product(x, out):
        total = None
        for k in range(SLOTS):
            part = dot(tiles_v[k], jnp.where(lane_slot == k, x, 0.0).astype(BF16), NN, None)
            total = part if total is None else total + part
        for q in range(NT):
            out[q] = total[q * TX : (q + 1) * TX]

    forward_product(jnp.ones((TILE, LANES), F32), tsend.at[0])
    trecv[0, j] = tsend[0, j]
    to_terms(3, lambda q: tsend.at[0, q], trecv.at[0], 0)

    slots_v[...] = jnp.concatenate([start_v[cols_s[k]] for k in range(SLOTS)], axis=0).T
    window = pl.ds(pl.multiple_of(128 * (i // 2), 128), 128)
    for g in range(TGROUPS):
        share_v[g] = start_v[g * 8 : (g + 1) * 8, :, window].reshape(LANES, 128).T
    half = pl.multiple_of(DX * lax.rem(i, 2), DX)
    start_share = jnp.concatenate([share_v[g, pl.ds(half, DX), :] for g in range(TGROUPS)], axis=0)
    e_v[...] = start_share

    arrived(0, d1_v, ND)
    arrived(1, cs_v, ND)
    cols_in = jnp.concatenate([d1_v[q, 0:8, :] for q in range(ND)], axis=0)
    sums_t = jnp.concatenate([cs_v[q] for q in range(ND)], axis=0).T
    same_col = jnp.where(cols_in == my_col[0:1, :], 1.0, 0.0)
    col_scale = lax.rsqrt(dot(sums_t, same_col, NN) + 1.0)
    arrived(2, m1_v, NT)
    gram = m1_v[0, 0:8, :]
    for q in range(1, NT):
        gram = gram + m1_v[q, 0:8, :]
    _, inverse0 = factor(unpacked(gram, 0))
    k0 = spread(inverse0)
    scaled_e = dot(slots_v[...], k0, NTR) * col_scale
    slots_v[...] = scaled_e
    forward_product(scaled_e, tsend.at[1])
    trecv[1, j] = tsend[1, j]
    to_terms(4, lambda q: tsend.at[1, q], trecv.at[1], 0)

    for q in range(NT):
        hit = iota((DOC_TILES * BLOCK, LANES), 0).astype(F32) == m1_v[q, 8:9, :]
        st_v[:, q * LANES : (q + 1) * LANES] = jnp.where(hit, 1.0, 0.0).astype(BF16)
    arrived(3, trecv.at[0], NT)

    def term_sum(n):
        flat = jnp.concatenate([trecv[n, q] for q in range(NT)], axis=1)
        return by_onehot(flat, st_v[...], NTR)

    def stacked(x, groups):
        return jnp.concatenate([x[:, g * LANES : (g + 1) * LANES] for g in range(groups)], axis=0)

    def flat_of(x, groups):
        n = x.shape[0] // groups
        return jnp.concatenate([x[g * n : (g + 1) * n] for g in range(groups)], axis=1)

    row_scale = stacked(lax.rsqrt(term_sum(0) + 1.0), DGROUPS)
    e_share = dot(e_v[...], k0, NTR)
    e_v[...] = e_share
    for q in range(ND):
        hit = iota((TERM_TILES * BLOCK, LANES), 0).astype(F32) == d1_v[q, 8:9, :]
        sd_v[:, q * LANES : (q + 1) * LANES] = jnp.where(hit, 1.0, 0.0).astype(BF16)
    cols_wide = jnp.concatenate([cols_in] * TGROUPS, axis=1)
    tile_at = (iota((ND * SLOTS, TERM_TILES * BLOCK), 1) // BLOCK).astype(F32)
    x_v[0:TILE, 0 : ND * SLOTS] = sums_t
    my_sums = x_v[pl.ds(pl.multiple_of(i * DX, DX), DX), 0 : ND * SLOTS]
    col_share = stacked(
        lax.rsqrt(dot(my_sums, jnp.where(cols_wide == tile_at, 1.0, 0.0), NN) + 1.0), TGROUPS
    )

    def all_sum(n, base, z):
        za[n, i] = z
        to_docs(base, lambda q: za.at[n, i], za.at[n], 0)

        def rest():
            arrived(base, za.at[n], ND)
            s = za[n, 0]
            for q in range(1, ND):
                s = s + za[n, q]
            zb[n, j] = s
            to_terms(base + 1, lambda q: zb.at[n, j], zb.at[n], 0)

        def last():
            arrived(base + 1, zb.at[n], NT)
            s = zb[n, 0]
            for q in range(1, NT):
                s = s + zb[n, q]
            return s

        return rest, last

    def term_gather(n, x):
        wide = by_onehot(flat_of(x, DGROUPS), st_v[...], NN)
        for q in range(NT):
            tsend[n, q] = wide[:, q * LANES : (q + 1) * LANES]

    arrived(4, trecv.at[1], NT)
    f1 = stacked(term_sum(1), DGROUPS) * row_scale
    rest, last = all_sum(0, 5, packed(fold(dot(f1, f1, TN)) * (1.0 / N_DOCS), None))
    term_gather(2, f1 * row_scale)
    trecv[2, j] = tsend[2, j]
    rest()
    to_terms(7, lambda q: tsend.at[2, q], trecv.at[2], 0)
    upper1, inverse1 = factor(unpacked(last(), 0))
    k1 = spread(inverse1)
    arrived(7, trecv.at[2], NT)
    pieces = jnp.concatenate([trecv[2, q] for q in range(NT)], axis=0)
    yt = dot(k1, pieces, NTR).astype(BF16)
    back = jnp.concatenate(
        [dot(yt[k * BLOCK : (k + 1) * BLOCK], tiles_v[k], NN, None) for k in range(SLOTS)], axis=0
    ).T
    for q in range(ND):
        dsend[0, q] = back[q * DX : (q + 1) * DX]
    drecv[0, i] = dsend[0, i]
    to_docs(8, lambda q: dsend.at[0, q], drecv.at[0], 0)

    u1 = dot(f1, k1, NTR)
    for g in range(DGROUPS):
        u_v[g] = u1[g * TX : (g + 1) * TX]
    p0 = upper1 * (N_DOCS / N_TERMS)
    expected = dot(e_share, spread(p0), NTR)

    arrived(8, drecv.at[0], ND)
    flat = jnp.concatenate([drecv[0, q] for q in range(ND)], axis=1)
    b1 = stacked(by_onehot(flat, sd_v[...], NTR), TGROUPS) * col_share - expected
    t2 = dot(b1, jnp.concatenate([b1, e_v[...]], axis=1), TN) * (1.0 / N_TERMS)
    rest, last = all_sum(1, 9, packed(fold(t2[:, :LANES]), fold(t2[:, LANES:])))
    for g in range(TGROUPS):
        share_v[g, 0:DX, :] = b1[g * DX : (g + 1) * DX]
    wide = by_onehot(flat_of(b1 * col_share, TGROUPS), sd_v[...], NN)
    for q in range(ND):
        dsend[1, q] = wide[:, q * LANES : (q + 1) * LANES]
    drecv[1, i] = dsend[1, i]
    to_docs(11, lambda q: dsend.at[1, q], drecv.at[1], 0)
    rest()
    z = last()
    r1 = unpacked(z, 2)
    pad = jnp.zeros((LANES - BLOCK, LANES), F32)
    g2 = unpacked(z, 0) - dot(r1, jnp.concatenate([r1, pad], axis=0), NTR)
    upper2, inverse2 = factor(g2)
    k2 = spread(inverse2)
    kr1 = spread(r1)
    arrived(11, drecv.at[1], ND)
    pieces = jnp.concatenate([drecv[1, q] for q in range(ND)], axis=0)
    pieces = pieces - dot(slots_v[...], kr1, NTR)
    forward_product(dot(pieces, k2, NTR), tsend.at[3])
    trecv[3, j] = tsend[3, j]
    to_terms(12, lambda q: tsend.at[3, q], trecv.at[3], 0)

    drecv[2, i] = share_v[i, 0:DX, :]
    to_docs(13, lambda q: share_v.at[q, pl.ds(0, DX), :], drecv.at[2], 0)
    trecv[4, j] = u_v[j // 4]
    to_terms(14, lambda q: u_v.at[q // 4], trecv.at[4], 0)
    p02 = upper2 * (N_TERMS / N_DOCS)
    expected = dot(u1, spread(p02), NTR)

    arrived(12, trecv.at[3], NT)
    f2 = stacked(term_sum(3), DGROUPS) * row_scale - expected
    t3 = dot(f2, jnp.concatenate([f2, u1], axis=1), TN) * (1.0 / N_DOCS)
    rest, last = all_sum(2, 15, packed(fold(t3[:, :LANES]), fold(t3[:, LANES:])))
    for g in range(DGROUPS):
        x_v[g * TX : (g + 1) * TX, :] = f2[g * TX : (g + 1) * TX]
    trecv[5, j] = x_v[pl.ds(pl.multiple_of((j // 4) * TX, TX), TX), :]
    to_terms(
        17, lambda q: x_v.at[pl.ds(pl.multiple_of((q // 4) * TX, TX), TX), :], trecv.at[5], 0
    )
    rest()

    arrived(13, drecv.at[2], ND)
    right_x = jnp.concatenate([drecv[2, q] for q in range(ND)], axis=0)
    start_st = start_v[pl.ds(i * 8, 8)].reshape(LANES, TILE)
    k20 = dot(k2, dot(kr1, k0, NN), NN)
    right = dot(k2, right_x, NTR) - dot(k20, start_st, NN)
    for g in range(8):
        right_o[:, g * TILE : (g + 1) * TILE] = right[g * BLOCK : (g + 1) * BLOCK]
    coef_o[0] = transposed(upper1)[:, :BLOCK]
    coef_o[1] = (p0 + r1)[:, :BLOCK]
    coef_o[2] = transposed(upper2)[:, :BLOCK]
    arrived(14, trecv.at[4], NT)
    left_u = jnp.concatenate([trecv[4, q] for q in range(NT)], axis=0)

    z = last()
    r2 = unpacked(z, 2)
    g3 = unpacked(z, 0) - dot(r2, jnp.concatenate([r2, pad], axis=0), NTR)
    upper3, inverse3 = factor(g3)
    arrived(17, trecv.at[5], NT)
    left_x = jnp.concatenate([trecv[5, q] for q in range(NT)], axis=0)
    left_x = left_x - dot(left_u, spread(r2), NTR)
    k3 = spread(inverse3)
    full = dot(k3, left_x, NTR)
    for m in range(4):
        tiles_two = full[m * 32 : (m + 1) * 32]

        @pl.when(lax.rem(j, 4) == m)
        def _():
            left_o[:, 0:TILE] = tiles_two[0:BLOCK]
            left_o[:, TILE : 2 * TILE] = tiles_two[BLOCK : 2 * BLOCK]

    coef_o[3] = (p02 + r2)[:, :BLOCK]
    coef_o[4] = transposed(upper3)[:, :BLOCK]
    for n, part in pending:
        pltpu.make_async_copy(part, part, send_sem.at[n]).wait()


def on_device(tiles, tile_rows, tile_cols, counts, start_block):
    smem = pl.BlockSpec(memory_space=pltpu.SMEM)
    anywhere = pl.BlockSpec(memory_space=pl.ANY)
    vmem = pl.BlockSpec(memory_space=pltpu.VMEM)
    return pl.pallas_call(
        kernel,
        out_shape=(
            jax.ShapeDtypeStruct((BLOCK, DOC_TILES * TILE // NT), F32),
            jax.ShapeDtypeStruct((BLOCK, TERM_TILES * TILE // ND), F32),
            jax.ShapeDtypeStruct((5, BLOCK, BLOCK), F32),
        ),
        in_specs=[smem, smem, smem, anywhere, anywhere],
        out_specs=(vmem, vmem, vmem),
        scratch_shapes=[
            pltpu.VMEM((SLOTS, TILE, TILE), BF16),
            pltpu.VMEM((TERM_TILES, BLOCK, TILE), F32),
            pltpu.VMEM((DOC_TILES * BLOCK, NT * LANES), BF16),
            pltpu.VMEM((TERM_TILES * BLOCK, ND * LANES), BF16),
            pltpu.VMEM((NT, 16, LANES), F32),
            pltpu.VMEM((ND, 16, LANES), F32),
            pltpu.VMEM((ND, SLOTS, TILE), F32),
            pltpu.VMEM((4, NT, TX, LANES), F32),
            pltpu.VMEM((6, NT, TX, LANES), F32),
            pltpu.VMEM((2, ND, DX, LANES), F32),
            pltpu.VMEM((3, ND, DX, LANES), F32),
            pltpu.VMEM((3, ND, 8, LANES), F32),
            pltpu.VMEM((3, NT, 8, LANES), F32),
            pltpu.VMEM((TILE, LANES), F32),
            pltpu.VMEM((TGROUPS, LANES, LANES), F32),
            pltpu.VMEM((TGROUPS * DX, LANES), F32),
            pltpu.VMEM((DGROUPS, TX, LANES), F32),
            pltpu.VMEM((TILE, LANES), F32),
            pltpu.SemaphoreType.DMA((SLOTS + 1,)),
            pltpu.SemaphoreType.DMA((18,)),
            pltpu.SemaphoreType.DMA((18,)),
        ],
        compiler_params=pltpu.CompilerParams(
            collective_id=0, has_side_effects=True, vmem_limit_bytes=60 * 1024 * 1024
        ),
    )(
        tile_rows.reshape(SLOTS),
        tile_cols.reshape(SLOTS),
        counts.reshape(1),
        tiles.reshape(SLOTS, TILE, TILE),
        start_block,
    )


def solution(mesh):
    return jax.shard_map(
        on_device,
        mesh=mesh,
        in_specs=(
            P("doc", "term", None, None, None),
            P("doc", "term", None),
            P("doc", "term", None),
            P("doc", "term"),
            P(None, "term"),
        ),
        out_specs=(P(None, ("doc", "term")), P(None, ("term", "doc")), P()),
        check_vma=False,
    )
```

time: 415 us -> 90.2 us (0.22)
  blocking collectives: 160 us -> 0 us
  waiting for transfers between devices: 113 us -> 0 us
  Pallas kernels: 0 us -> 84.1 us
  starting transfers between devices: 40.4 us -> 0 us
  matrix products: 35.2 us -> 0 us
  local copies, waits for them, and re-layouts: 37.4 us -> 4.54 us
  other arithmetic: 24.5 us -> 0 us
    psum x25 -> x0, blocking collectives: 160 us -> none  [by_axis(): return functools.reduce(lax.psum, axes, shard)]
    all_to_all x8 -> x0, waiting for transfers between devices: 113 us -> none  [the longest x3 58.6 us: sent_and_summed(): lax.all_to_all(pieces, axis, split_axis=0, concat_axis=0, tiled=True)]
    pallas_call x0 -> x1, Pallas kernels: none -> 84.1 us  [on_device(): pl.pallas_call(kernel, out_shape=(jax.ShapeDtypeStruct((BLOCK, DOC_TILES...]
    all_to_all x8 -> x0, starting transfers between devices: 40.4 us -> none  [the longest x5 26.6 us: sent_to_all(): lax.all_to_all(jnp.broadcast_to(shard[None], (peers, *shard.shape)), axis...]
    dot_general x21 -> x0, matrix products: 30.3 us -> none  [the longest x2 4.6 us: forward(): jnp.einsum('kab,kcb->kca', local_tiles, pieces, preferred_element_type=jn...]
    another operation x21 -> x0, other arithmetic: 16.7 us -> none  [the longest x9 6.45 us: orthonormal(): factor = jnp.linalg.cholesky(gram_matrix)]
    another operation x6 -> x0, local copies, waits for them, and re-layouts: 16.4 us -> none  [cut_along(): shard.reshape(*lengths[:dim], peers, lengths[dim] // peers, *lengths[dim...]
    broadcast_in_dim x5 -> x0, local copies, waits for them, and re-layouts: 5.95 us -> none  [sent_to_all(): jnp.broadcast_to(shard[None], (peers, *shard.shape))]
  transfers between devices with their start and end apart: 8 -> 0, of which waited for: 8 -> 0; matrix products, arithmetic and copies ran while one was open for 7% -> 0% of each run, Pallas kernels for 0% -> 0%
where the time goes in v1:
time: 90.2 us; the launch traced here: 89.9 us
  Pallas kernels  84.1 us (93%)
  local copies, waits for them, and re-layouts  4.54 us (5%)
  between operations  1.29 us (1%)
    pallas_call x1, Pallas kernels, on_device(): pl.pallas_call(kernel, out_shape=(jax.ShapeDtypeStruct((BLOCK, DOC_TILES...  84.1 us
    unnamed x3, local copies, waits for them, and re-layouts  4.54 us

profile of v1, /device:TPU:1, one launch (start us, length us, event | category | flops | bytes accessed | tf_op | source)
XLA Modules:
  0.0 89.9 jit_solution(538511940069885458)
XLA Ops:
  1.3 84.1 %shard_map.76 = (f32[16,1024]{1,0:T(8,128)}, f32[16,4096]{1,0:T(8,128)}, f32[5,16,16]{2,1,0:T(8,128)}) custom-call(s32[8]{0:T(128)} %bitcast.6, s32[8]{0:T(128)} %bitcast.7, s32[1]{0:T(128)} %bitcast.4.cnt_s, bf16[8,512,512]{2,1,0:T(8,128)(2,1)} %bitcast.5, f32[16,32768]{1,0:T(8,128)} %start_h.1), custom_call_target="tpu_custom_call" | custom-call | tf_op jit(solution)/shard_map/pallas_call | solution.py:421
  85.4 1.5 %copy.12 = f32[16,1024]{1,0:T(8,128)} copy(f32[16,1024]{1,0:T(8,128)} %get-tuple-element.6) | data formatting | bytes 131072
  86.8 1.7 %copy.13 = f32[16,4096]{1,0:T(8,128)} copy(f32[16,4096]{1,0:T(8,128)} %get-tuple-element.7) | data formatting | bytes 524288
  88.5 1.4 %copy.14 = f32[5,16,16]{2,1,0:T(8,128)} copy(f32[5,16,16]{2,1,0:T(8,128)} %get-tuple-element.8) | data formatting | bytes 10240

commit v2 on v1

v2 whole, which is shorter than its diff:
```python
import functools

import jax
import jax.numpy as jnp
from jax import lax
from jax.experimental import pallas as pl
from jax.experimental.pallas import tpu as pltpu
from jax.sharding import PartitionSpec as P

MESH = pl.DeviceIdType.MESH
F32 = jnp.float32
BF16 = jnp.bfloat16
TILE = 512
BLOCK = 16
SLOTS = 8
LANES = SLOTS * BLOCK
TERM_TILES = 64
DOC_TILES = 32
ND = 8
NT = 16
DX = TILE // ND
TX = TILE // NT
DGROUPS = DOC_TILES * BLOCK // LANES
TGROUPS = TERM_TILES * BLOCK // LANES
N_DOCS = ND * DOC_TILES * TILE
N_TERMS = NT * TERM_TILES * TILE
HIGHEST = lax.Precision.HIGHEST


def dot(a, b, contract, precision=HIGHEST):
    return lax.dot_general(
        a, b, (contract, ((), ())), precision=precision, preferred_element_type=F32
    )


NN = ((1,), (0,))
NTR = ((1,), (1,))
TN = ((0,), (0,))


def halves(x):
    hi = x.astype(BF16)
    lo = (x - hi.astype(F32)).astype(BF16)
    return jnp.concatenate([hi, lo], axis=0)


def by_onehot(x, onehot, contract):
    n = x.shape[0]
    both = dot(halves(x), onehot, contract, None)
    return both[:n] + both[n:]


def iota(shape, dim):
    return lax.broadcasted_iota(jnp.int32, shape, dim)


def roll(x, shift):
    return pltpu.roll(x, shift, 1)


def fold(t):
    same = iota((LANES, LANES), 0) // BLOCK == iota((LANES, LANES), 1) // BLOCK
    t = jnp.where(same, t, 0.0)
    w = t[0:BLOCK]
    for g in range(1, SLOTS):
        w = w + t[g * BLOCK : (g + 1) * BLOCK]
    w = w + roll(w, 64)
    w = w + roll(w, 32)
    return w + roll(w, 16)


def packed(s, r):
    group = iota((8, LANES), 1) // BLOCK
    z = jnp.where(group == 0, s[0:8], s[8:16])
    if r is None:
        return z
    return jnp.where(group < 2, z, jnp.where(group == 2, r[0:8], r[8:16]))


def unpacked(z, first):
    lane = iota((BLOCK, LANES), 1)
    top = z if first == 0 else roll(z, LANES - BLOCK * first)
    low = roll(z, LANES - BLOCK * (first + 1))
    return jnp.where(lane < BLOCK, jnp.concatenate([top, low], axis=0), 0.0)


def spread(m):
    same = iota((LANES, LANES), 0) // BLOCK == iota((LANES, LANES), 1) // BLOCK
    r = m + roll(m, 16)
    r = r + roll(r, 32)
    r = r + roll(r, 64)
    return jnp.where(same, jnp.concatenate([r] * SLOTS, axis=0), 0.0)


def factor(s):
    lane = iota((BLOCK, LANES), 1)
    sub = iota((BLOCK, LANES), 0)
    m = jnp.where(lane < BLOCK, s, jnp.where(lane == sub + BLOCK, 1.0, 0.0))
    for c in range(BLOCK - 1):
        ratio = m[c : c + 1, :] / m[c : c + 1, c : c + 1]
        m = m - jnp.where(sub > c, m[:, c : c + 1], 0.0) * ratio
    diag = jnp.sum(jnp.where(lane == sub, m, 0.0), axis=1, keepdims=True)
    m = m * lax.rsqrt(diag)
    upper = jnp.where((lane < BLOCK) & (lane >= sub), m, 0.0)
    inverse = jnp.where(lane < BLOCK, roll(m, LANES - BLOCK), 0.0)
    return upper, inverse


def transposed(m):
    full = jnp.concatenate([m, jnp.zeros((LANES - BLOCK, LANES), F32)], axis=0)
    return full.T[:BLOCK, :]


def kernel(
    cnt_h, rows_h, cols_h, tiles_h, start_h,
    left_o, right_o, coef_o,
    cnt_s, rows_s, cols_s, tiles_v, start_v, st_v, sd_v,
    m1_v, d1_v, cs_v,
    tsend, trecv, dsend, drecv, za, zb,
    slots_v, share_v, cst_v, f0_v, x2_v,
    load_sem, send_sem, recv_sem,
):
    i = lax.axis_index("doc")
    j = lax.axis_index("term")
    bar = pltpu.get_barrier_semaphore()
    for d in range(1, NT):
        pl.semaphore_signal(bar, 1, device_id=(i, lax.rem(j + d, NT)), device_id_type=MESH)
    for d in range(1, ND):
        pl.semaphore_signal(bar, 1, device_id=(lax.rem(i + d, ND), j), device_id_type=MESH)

    def load_start(t, carry):
        columns = pl.ds(pl.multiple_of(t * TILE, TILE), TILE)
        pltpu.make_async_copy(start_h.at[:, columns], start_v.at[t], load_sem.at[SLOTS]).start()
        return carry

    lax.fori_loop(0, TERM_TILES, load_start, 0)
    rows_load = pltpu.make_async_copy(rows_h, rows_s, load_sem.at[SLOTS + 1])
    cols_load = pltpu.make_async_copy(cols_h, cols_s, load_sem.at[SLOTS + 2])
    cnt_load = pltpu.make_async_copy(cnt_h, cnt_s, load_sem.at[SLOTS + 3])
    cnt_load.start()
    rows_load.start()
    cols_load.start()
    loads = []
    for k in range(SLOTS):
        load = pltpu.make_async_copy(tiles_h.at[k], tiles_v.at[k], load_sem.at[k])
        load.start()
        loads.append(load)

    pending = []

    def to_terms(n, src_of, dst):
        def send(d, carry):
            q = lax.rem(j + d, NT)
            pltpu.make_async_remote_copy(
                src_ref=src_of(q), dst_ref=dst.at[j],
                send_sem=send_sem.at[n], recv_sem=recv_sem.at[n],
                device_id=(i, q), device_id_type=MESH,
            ).start()
            return carry
        lax.fori_loop(1, NT, send, 0)
        pending.append((n, dst.at[pl.ds(0, NT - 1)]))

    def to_docs(n, src_of, dst):
        def send(d, carry):
            q = lax.rem(i + d, ND)
            pltpu.make_async_remote_copy(
                src_ref=src_of(q), dst_ref=dst.at[i],
                send_sem=send_sem.at[n], recv_sem=recv_sem.at[n],
                device_id=(q, j), device_id_type=MESH,
            ).start()
            return carry
        lax.fori_loop(1, ND, send, 0)
        pending.append((n, dst.at[pl.ds(0, ND - 1)]))

    def arrived(n, dst, peers):
        part = dst.at[pl.ds(0, peers - 1)]
        pltpu.make_async_copy(part, part, recv_sem.at[n]).wait()

    def term_exchange(n, slot, total):
        for q in range(NT):
            tsend[slot, q] = total[q * TX : (q + 1) * TX]
        trecv[slot, j] = tsend[slot, j]
        to_terms(n, lambda q: tsend.at[slot, q], trecv.at[slot])

    def doc_exchange(n, slot, total):
        for q in range(ND):
            dsend[slot, q] = total[q * DX : (q + 1) * DX]
        drecv[slot, i] = dsend[slot, i]
        to_docs(n, lambda q: dsend.at[slot, q], drecv.at[slot])

    def forward_product(x):
        lane_slot = iota((TILE, LANES), 1) // BLOCK
        total = None
        for k in range(SLOTS):
            masked = [jnp.where(lane_slot == k, part, 0.0).astype(BF16) for part in x]
            weights = masked[0] if len(masked) == 1 else jnp.concatenate(masked, axis=1)
            part = dot(tiles_v[k], weights, NN, None)
            total = part if total is None else total + part
        if len(x) == 2:
            total = total[:, :LANES] + total[:, LANES:]
        return total

    def split(x):
        hi = x.astype(BF16).astype(F32)
        return [hi, x - hi]

    def stacked(x, groups):
        return jnp.concatenate([x[:, g * LANES : (g + 1) * LANES] for g in range(groups)], axis=0)

    def flat_of(x, groups):
        n = x.shape[0] // groups
        return jnp.concatenate([x[g * n : (g + 1) * n] for g in range(groups)], axis=1)

    def term_sum(slot):
        flat = jnp.concatenate([trecv[slot, q] for q in range(NT)], axis=1)
        return by_onehot(flat, st_v[...], NTR)

    def all_sum(n, base, z):
        za[n, i] = z
        to_docs(base, lambda q: za.at[n, i], za.at[n])

        def rest():
            arrived(base, za.at[n], ND)
            s = za[n, 0]
            for q in range(1, ND):
                s = s + za[n, q]
            zb[n, j] = s
            to_terms(base + 1, lambda q: zb.at[n, j], zb.at[n])

        def last():
            arrived(base + 1, zb.at[n], NT)
            s = zb[n, 0]
            for q in range(1, NT):
                s = s + zb[n, q]
            return s

        return rest, last

    pltpu.make_async_copy(start_v, start_v, load_sem.at[SLOTS]).wait()
    acc = jnp.zeros((2 * LANES, 2 * LANES), F32)
    for ch in range(8):
        both = halves(start_v[ch * 8 : (ch + 1) * 8].reshape(LANES, TILE))
        acc = acc + dot(both, both, NTR, None)
    t = acc[:LANES, :LANES] + acc[:LANES, LANES:] + acc[LANES:, :LANES] + acc[LANES:, LANES:]
    start_gram = packed(fold(t) * (1.0 / N_TERMS), None)

    cnt_load.wait()
    rows_load.wait()
    cols_load.wait()
    lane8 = iota((8, LANES), 1)
    sub8 = iota((8, LANES), 0)
    cnt = cnt_s[0, 0]
    row_at = jnp.zeros((8, LANES), jnp.int32)
    my_col = jnp.zeros((8, LANES), jnp.int32)
    col_of = jnp.zeros((8, LANES), jnp.int32)
    for k in range(SLOTS):
        here = lane8 // BLOCK == k
        row_at = jnp.where(here, rows_s[0, k] * BLOCK, row_at)
        my_col = jnp.where(here, cols_s[0, k], my_col)
        col_of = jnp.where(sub8 == k, cols_s[0, k], col_of)
    row_at = jnp.where(lane8 // BLOCK < cnt, row_at, -100000)
    my_col = jnp.where(lane8 // BLOCK < cnt, my_col, -10000)
    col_of = jnp.where(sub8 < cnt, col_of, -10000)
    col_at = my_col * BLOCK
    row_at = (row_at + lane8 % BLOCK).astype(F32)
    col_at = (col_at + lane8 % BLOCK).astype(F32)
    my_col = my_col.astype(F32)
    d1_v[i] = jnp.concatenate([col_of.astype(F32), col_at], axis=0)
    m1_v[j] = jnp.concatenate([start_gram, row_at], axis=0)

    col_sums = jnp.zeros((16, TILE), F32)
    for k in range(SLOTS):
        loads[k].wait()
        ones = jnp.where(iota((16, TILE), 0) == k, 1.0, 0.0).astype(BF16)
        col_sums = col_sums + dot(ones, tiles_v[k], NN, None)
    cs_v[i] = col_sums[:SLOTS]

    pl.semaphore_wait(bar, ND - 1 + NT - 1)
    to_docs(0, lambda q: d1_v.at[i], d1_v)
    to_docs(1, lambda q: cs_v.at[i], cs_v)
    to_terms(2, lambda q: m1_v.at[j], m1_v)

    term_exchange(3, 0, forward_product([jnp.ones((TILE, LANES), F32)]))
    slots_t = jnp.concatenate([start_v[cols_s[0, k]] for k in range(SLOTS)], axis=0).T
    slots_v[...] = slots_t

    arrived(0, d1_v, ND)
    arrived(1, cs_v, ND)
    cols_in = jnp.concatenate([d1_v[q, 0:8, :] for q in range(ND)], axis=0)
    sums_t = jnp.concatenate([cs_v[q] for q in range(ND)], axis=0).T
    cst_v[...] = sums_t
    same_col = jnp.where(cols_in == my_col[0:1, :], 1.0, 0.0)
    col_scale = lax.rsqrt(dot(sums_t, same_col, NN) + 1.0)
    scaled_slots = slots_v[...] * col_scale
    arrived(2, m1_v, NT)
    gram = m1_v[0, 0:8, :]
    for q in range(1, NT):
        gram = gram + m1_v[q, 0:8, :]
    _, inverse0 = factor(unpacked(gram, 0))
    k0 = spread(inverse0)
    term_exchange(4, 1, forward_product([dot(scaled_slots, k0, NTR)]))

    for q in range(NT):
        hit = iota((DOC_TILES * BLOCK, LANES), 0).astype(F32) == m1_v[q, 8:9, :]
        st_v[:, q * LANES : (q + 1) * LANES] = jnp.where(hit, 1.0, 0.0).astype(BF16)
    arrived(3, trecv.at[0], NT)
    row_scale = lax.rsqrt(term_sum(0) + 1.0)
    row_square = row_scale * row_scale

    arrived(4, trecv.at[1], NT)
    image = term_sum(1)
    wide = by_onehot(image * row_square, st_v[...], NN)
    for q in range(NT):
        tsend[2, q] = wide[:, q * LANES : (q + 1) * LANES]
    trecv[2, j] = tsend[2, j]
    to_terms(5, lambda q: tsend.at[2, q], trecv.at[2])
    f0 = stacked(image * row_scale, DGROUPS)
    rest, last = all_sum(0, 6, packed(fold(dot(f0, f0, TN)) * (1.0 / N_DOCS), None))
    for g in range(DGROUPS):
        f0_v[g] = f0[g * TX : (g + 1) * TX]
    trecv[4, j] = f0_v[j // 4]
    to_terms(8, lambda q: f0_v.at[q // 4], trecv.at[4])

    for q in range(ND):
        hit = iota((TERM_TILES * BLOCK, LANES), 0).astype(F32) == d1_v[q, 8:9, :]
        sd_v[:, q * LANES : (q + 1) * LANES] = jnp.where(hit, 1.0, 0.0).astype(BF16)
    rest()
    arrived(5, trecv.at[2], NT)
    pieces = jnp.concatenate([trecv[2, q] for q in range(NT)], axis=0).T
    hi = pieces.astype(BF16)
    lo = (pieces - hi.astype(F32)).astype(BF16)
    back = []
    for k in range(SLOTS):
        cut = slice(k * BLOCK, (k + 1) * BLOCK)
        both = dot(jnp.concatenate([hi[cut], lo[cut]], axis=0), tiles_v[k], NN, None)
        back.append(both[:BLOCK] + both[BLOCK:])
    doc_exchange(9, 0, jnp.concatenate(back, axis=0).T)

    cols_wide = jnp.concatenate([cols_in] * TGROUPS, axis=1)
    tile_at = (iota((ND * SLOTS, TERM_TILES * BLOCK), 1) // BLOCK).astype(F32)
    my_sums = cst_v[pl.ds(pl.multiple_of(i * DX, DX), DX), :]
    col_share = lax.rsqrt(dot(my_sums, jnp.where(cols_wide == tile_at, 1.0, 0.0), NN) + 1.0)
    col_square = col_share * col_share
    window = pl.ds(pl.multiple_of(128 * (i // 2), 128), 128)
    for g in range(TGROUPS):
        share_v[g] = start_v[g * 8 : (g + 1) * 8, :, window].reshape(LANES, 128).T
    half = pl.multiple_of(DX * lax.rem(i, 2), DX)
    start_share = jnp.concatenate([share_v[g, pl.ds(half, DX), :] for g in range(TGROUPS)], axis=0)
    e_share = dot(start_share, k0, NTR)
    upper1, inverse1 = factor(unpacked(last(), 0))
    k1 = spread(inverse1)
    p0 = upper1 * (N_DOCS / N_TERMS)
    expected = dot(e_share, spread(p0), NTR)
    u1 = dot(f0, k1, NTR)

    arrived(9, drecv.at[0], ND)
    flat = jnp.concatenate([drecv[0, q] for q in range(ND)], axis=1)
    image = by_onehot(flat, sd_v[...], NTR)
    wide = by_onehot(image * col_square, sd_v[...], NN)
    for q in range(ND):
        dsend[1, q] = wide[:, q * LANES : (q + 1) * LANES]
    drecv[1, i] = dsend[1, i]
    to_docs(10, lambda q: dsend.at[1, q], drecv.at[1])
    b1 = dot(stacked(image * col_share, TGROUPS), k1, NTR) - expected
    t2 = dot(b1, jnp.concatenate([b1, e_share], axis=1), TN) * (1.0 / N_TERMS)
    rest, last = all_sum(1, 11, packed(fold(t2[:, :LANES]), fold(t2[:, LANES:])))
    for g in range(TGROUPS):
        share_v[g, 0:DX, :] = b1[g * DX : (g + 1) * DX]
    drecv[2, i] = share_v[i, 0:DX, :]
    to_docs(13, lambda q: share_v.at[q, pl.ds(0, DX), :], drecv.at[2])

    arrived(10, drecv.at[1], ND)
    pieces = jnp.concatenate([drecv[1, q] for q in range(ND)], axis=0)
    term_exchange(14, 3, forward_product(split(pieces)))
    rest()
    z = last()
    r1 = unpacked(z, 2)
    pad = jnp.zeros((LANES - BLOCK, LANES), F32)
    g2 = unpacked(z, 0) - dot(r1, jnp.concatenate([r1, pad], axis=0), NTR)
    upper2, inverse2 = factor(g2)
    k2 = spread(inverse2)
    kr1 = spread(r1)
    p02 = upper2 * (N_TERMS / N_DOCS)
    k21 = dot(k2, k1, NN)
    known = dot(k2, spread(p0 + r1), NN) + dot(spread(p02), k1, NN)
    expected = dot(f0, known, NTR)

    arrived(14, trecv.at[3], NT)
    image = term_sum(3) * row_scale
    x2 = dot(stacked(image, DGROUPS), k21, NTR) - expected
    t3 = dot(x2, jnp.concatenate([x2, u1], axis=1), TN) * (1.0 / N_DOCS)
    rest, last = all_sum(2, 15, packed(fold(t3[:, :LANES]), fold(t3[:, LANES:])))
    for g in range(DGROUPS):
        x2_v[g] = x2[g * TX : (g + 1) * TX]
    trecv[5, j] = x2_v[j // 4]
    to_terms(17, lambda q: x2_v.at[q // 4], trecv.at[5])
    arrived(13, drecv.at[2], ND)
    right_x = jnp.concatenate([drecv[2, q] for q in range(ND)], axis=0)
    rest()

    start_st = start_v[pl.ds(i * 8, 8)].reshape(LANES, TILE)
    k20 = dot(k2, dot(kr1, k0, NN), NN)
    right = dot(k2, right_x, NTR) - dot(k20, start_st, NN)
    for g in range(8):
        right_o[:, g * TILE : (g + 1) * TILE] = right[g * BLOCK : (g + 1) * BLOCK]
    coef_o[0] = transposed(upper1)[:, :BLOCK]
    coef_o[1] = (p0 + r1)[:, :BLOCK]
    coef_o[2] = transposed(upper2)[:, :BLOCK]
    arrived(8, trecv.at[4], NT)
    left_u = dot(jnp.concatenate([trecv[4, q] for q in range(NT)], axis=0), k1, NTR)
    arrived(17, trecv.at[5], NT)
    left_x = jnp.concatenate([trecv[5, q] for q in range(NT)], axis=0)

    z = last()
    r2 = unpacked(z, 2)
    g3 = unpacked(z, 0) - dot(r2, jnp.concatenate([r2, pad], axis=0), NTR)
    upper3, inverse3 = factor(g3)
    left_x = left_x - dot(left_u, spread(r2), NTR)
    rep = inverse3 + roll(inverse3, 16)
    rep = rep + roll(rep, 32)
    rep = rep + roll(rep, 64)
    mine = iota((2 * BLOCK, LANES), 1) // BLOCK == iota((2 * BLOCK, LANES), 0) // BLOCK + 2 * lax.rem(j, 4)
    left = dot(jnp.where(mine, jnp.concatenate([rep, rep], axis=0), 0.0), left_x, NTR)
    left_o[:, 0:TILE] = left[0:BLOCK]
    left_o[:, TILE : 2 * TILE] = left[BLOCK : 2 * BLOCK]
    coef_o[3] = (p02 + r2)[:, :BLOCK]
    coef_o[4] = transposed(upper3)[:, :BLOCK]
    for n, part in pending:
        pltpu.make_async_copy(part, part, send_sem.at[n]).wait()


def hand_over(left_i, right_i, coef_i, left_o, right_o, coef_o):
    left_o[...] = left_i[...]
    right_o[...] = right_i[...]
    coef_o[...] = coef_i[...]


def on_device(tiles, tile_rows, tile_cols, counts, start_block):
    anywhere = pl.BlockSpec(memory_space=pl.ANY)
    vmem = pl.BlockSpec(memory_space=pltpu.VMEM)
    shapes = (
        jax.ShapeDtypeStruct((BLOCK, DOC_TILES * TILE // NT), F32),
        jax.ShapeDtypeStruct((BLOCK, TERM_TILES * TILE // ND), F32),
        jax.ShapeDtypeStruct((5, BLOCK, BLOCK), F32),
    )
    results = pl.pallas_call(
        kernel,
        out_shape=shapes,
        in_specs=[anywhere] * 5,
        out_specs=(vmem, vmem, vmem),
        scratch_shapes=[
            pltpu.SMEM((1, 1), jnp.int32),
            pltpu.SMEM((1, SLOTS), jnp.int32),
            pltpu.SMEM((1, SLOTS), jnp.int32),
            pltpu.VMEM((SLOTS, TILE, TILE), BF16),
            pltpu.VMEM((TERM_TILES, BLOCK, TILE), F32),
            pltpu.VMEM((DOC_TILES * BLOCK, NT * LANES), BF16),
            pltpu.VMEM((TERM_TILES * BLOCK, ND * LANES), BF16),
            pltpu.VMEM((NT, 16, LANES), F32),
            pltpu.VMEM((ND, 16, LANES), F32),
            pltpu.VMEM((ND, SLOTS, TILE), F32),
            pltpu.VMEM((4, NT, TX, LANES), F32),
            pltpu.VMEM((6, NT, TX, LANES), F32),
            pltpu.VMEM((2, ND, DX, LANES), F32),
            pltpu.VMEM((3, ND, DX, LANES), F32),
            pltpu.VMEM((3, ND, 8, LANES), F32),
            pltpu.VMEM((3, NT, 8, LANES), F32),
            pltpu.VMEM((TILE, LANES), F32),
            pltpu.VMEM((TGROUPS, LANES, LANES), F32),
            pltpu.VMEM((TILE, ND * SLOTS), F32),
            pltpu.VMEM((DGROUPS, TX, LANES), F32),
            pltpu.VMEM((DGROUPS, TX, LANES), F32),
            pltpu.SemaphoreType.DMA((SLOTS + 4,)),
            pltpu.SemaphoreType.DMA((18,)),
            pltpu.SemaphoreType.DMA((18,)),
        ],
        compiler_params=pltpu.CompilerParams(
            collective_id=0, has_side_effects=True, vmem_limit_bytes=65000000
        ),
    )(
        counts,
        tile_rows.reshape(1, SLOTS),
        tile_cols.reshape(1, SLOTS),
        tiles.reshape(SLOTS, TILE, TILE),
        start_block,
    )
    return pl.pallas_call(
        hand_over,
        out_shape=shapes,
        in_specs=[vmem, vmem, vmem],
        out_specs=(vmem, vmem, vmem),
        compiler_params=pltpu.CompilerParams(vmem_limit_bytes=8 * 1024 * 1024),
    )(*results)


def solution(mesh):
    return jax.shard_map(
        on_device,
        mesh=mesh,
        in_specs=(
            P("doc", "term", None, None, None),
            P("doc", "term", None),
            P("doc", "term", None),
            P("doc", "term"),
            P(None, "term"),
        ),
        out_specs=(P(None, ("doc", "term")), P(None, ("term", "doc")), P()),
        check_vma=False,
    )
```

time: 90.2 us -> 82 us (0.909)
  Pallas kernels: 84.1 us -> 77.9 us
  local copies, waits for them, and re-layouts: 4.54 us -> 2.56 us
    pallas_call x1 -> x2, Pallas kernels: 84.1 us -> 77.9 us  [the longest x1 77.1 us: on_device(): pl.pallas_call(kernel, out_shape=shapes, in_specs=[anywhere] * 5, out_spe...]
    unnamed x3 -> x6, local copies, waits for them, and re-layouts: 4.54 us -> 2.56 us
where the time goes in v2:
time: 82 us; the launch traced here: 81.7 us
  Pallas kernels  77.9 us (95%)
  local copies, waits for them, and re-layouts  2.56 us (3%)
  between operations  1.3 us (2%)
    pallas_call x1, Pallas kernels, on_device(): pl.pallas_call(kernel, out_shape=shapes, in_specs=[anywhere] * 5, out_spe...  77.1 us
    unnamed x6, local copies, waits for them, and re-layouts  2.56 us

profile of v2, /device:TPU:1, one launch (start us, length us, event | category | flops | bytes accessed | tf_op | source)
XLA Modules:
  0.0 81.7 jit_solution(11198469832884201236)
XLA Ops:
  1.3 77.1 %shard_map.76 = (f32[16,1024]{1,0:T(8,128)}, f32[16,4096]{1,0:T(8,128)}, f32[5,16,16]{2,1,0:T(8,128)}) custom-call(s32[1,1]{1,0:T(1,128)S(6)} %copy.8.cnt_h, s32[1,8]{1,0:T(1,128)} %bitcast.4, s32[1,8]{1,0:T(1,128)} %bitcast.5, bf16[8,512,512]{2,1,0:T(8,128)(2,1)} %bitcast.3, f32[16,32768]{1,0:T(8,128)} %start_h.1), custom_call_target="tpu_custom_call" | custom-call | tf_op jit(solution)/shard_map/pallas_call | solution.py:446
  78.4 0.0 copy-start
  78.4 0.9 %copy-done = f32[16,4096]{1,0:T(8,128)S(1)} copy-done((f32[16,4096]{1,0:T(8,128)S(1)}, f32[16,4096]{1,0:T(8,128)}, u32[]{:S(2)}) %copy-start) | copy-done | bytes 262168
  79.4 0.0 copy-start.1
  79.4 0.8 %copy-done.1 = f32[16,1024]{1,0:T(8,128)S(1)} copy-done((f32[16,1024]{1,0:T(8,128)S(1)}, f32[16,1024]{1,0:T(8,128)}, u32[]{:S(2)}) %copy-start.1) | copy-done | bytes 65560
  80.2 0.0 copy-start.2
  80.2 0.8 copy-done.2
  81.0 0.7 shard_map.77
Async XLA Ops:
  78.4 1.0 %copy-start = (f32[16,4096]{1,0:T(8,128)S(1)}, f32[16,4096]{1,0:T(8,128)}, u32[]{:S(2)}) copy-start(f32[16,4096]{1,0:T(8,128)} %get-tuple-element.7.right_i) | copy-start | bytes 786436
  79.4 0.8 %copy-start.1 = (f32[16,1024]{1,0:T(8,128)S(1)}, f32[16,1024]{1,0:T(8,128)}, u32[]{:S(2)}) copy-start(f32[16,1024]{1,0:T(8,128)} %get-tuple-element.6.left_i) | copy-start | bytes 196612
  80.2 0.8 copy-start.2

commit v3 on v2

--- a/solution.py
+++ b/solution.py
@@ -117,7 +117,7 @@
     cnt_s, rows_s, cols_s, tiles_v, start_v, st_v, sd_v,
     m1_v, d1_v, cs_v,
     tsend, trecv, dsend, drecv, za, zb,
-    slots_v, share_v, cst_v, f0_v, x2_v,
+    slots_v, share_v, cst_v, rs_v, rsr_v, rst_v, pk_v, pkr_v,
     load_sem, send_sem, recv_sem,
 ):
     i = lax.axis_index("doc")
@@ -211,6 +211,25 @@
         n = x.shape[0] // groups
         return jnp.concatenate([x[g * n : (g + 1) * n] for g in range(groups)], axis=1)
 
+    def pack(x, out):
+        group = iota((8, LANES), 1) // (2 * BLOCK)
+        for g in range(DGROUPS):
+            rows = [x[g * TX + 8 * h : g * TX + 8 * (h + 1)] for h in range(4)]
+            for m in range(4):
+                total = None
+                for h in range(4):
+                    shift = (32 * (h - m)) % LANES
+                    turned = rows[h] if shift == 0 else roll(rows[h], shift)
+                    total = turned if total is None else jnp.where(group == h, turned, total)
+                out[4 * g + m] = total
+
+    def unpack(ref):
+        rows = []
+        for q in range(NT):
+            for h in range(4):
+                rows.append(ref[q] if h == 0 else roll(ref[q], LANES - 32 * h))
+        return jnp.concatenate(rows, axis=0)
+
     def term_sum(slot):
         flat = jnp.concatenate([trecv[slot, q] for q in range(NT)], axis=1)
         return by_onehot(flat, st_v[...], NTR)
@@ -253,20 +272,23 @@
     row_at = jnp.zeros((8, LANES), jnp.int32)
     my_col = jnp.zeros((8, LANES), jnp.int32)
     col_of = jnp.zeros((8, LANES), jnp.int32)
+    row_of = jnp.zeros((8, LANES), jnp.int32)
     for k in range(SLOTS):
         here = lane8 // BLOCK == k
         row_at = jnp.where(here, rows_s[0, k] * BLOCK, row_at)
         my_col = jnp.where(here, cols_s[0, k], my_col)
         col_of = jnp.where(sub8 == k, cols_s[0, k], col_of)
+        row_of = jnp.where(sub8 == k, rows_s[0, k], row_of)
     row_at = jnp.where(lane8 // BLOCK < cnt, row_at, -100000)
     my_col = jnp.where(lane8 // BLOCK < cnt, my_col, -10000)
     col_of = jnp.where(sub8 < cnt, col_of, -10000)
+    row_of = jnp.where(sub8 < cnt, row_of, -10000)
     col_at = my_col * BLOCK
     row_at = (row_at + lane8 % BLOCK).astype(F32)
     col_at = (col_at + lane8 % BLOCK).astype(F32)
     my_col = my_col.astype(F32)
     d1_v[i] = jnp.concatenate([col_of.astype(F32), col_at], axis=0)
-    m1_v[j] = jnp.concatenate([start_gram, row_at], axis=0)
+    m1_v[j] = jnp.concatenate([start_gram, row_at, row_of.astype(F32)], axis=0)
 
     col_sums = jnp.zeros((16, TILE), F32)
     for k in range(SLOTS):
@@ -280,7 +302,14 @@
     to_docs(1, lambda q: cs_v.at[i], cs_v)
     to_terms(2, lambda q: m1_v.at[j], m1_v)
 
-    term_exchange(3, 0, forward_product([jnp.ones((TILE, LANES), F32)]))
+    row_sums = jnp.zeros((16, TILE), F32)
+    for k in range(SLOTS):
+        ones = jnp.where(iota((16, TILE), 0) == k, 1.0, 0.0).astype(BF16)
+        row_sums = row_sums + dot(ones, tiles_v[k], NTR, None)
+    for g in range(DGROUPS):
+        rs_v[g] = row_sums[:SLOTS, g * LANES : (g + 1) * LANES]
+    rsr_v[j] = rs_v[j // 4]
+    to_terms(3, lambda q: rs_v.at[q // 4], rsr_v)
     slots_t = jnp.concatenate([start_v[cols_s[0, k]] for k in range(SLOTS)], axis=0).T
     slots_v[...] = slots_t
 
@@ -303,8 +332,14 @@
     for q in range(NT):
         hit = iota((DOC_TILES * BLOCK, LANES), 0).astype(F32) == m1_v[q, 8:9, :]
         st_v[:, q * LANES : (q + 1) * LANES] = jnp.where(hit, 1.0, 0.0).astype(BF16)
-    arrived(3, trecv.at[0], NT)
-    row_scale = lax.rsqrt(term_sum(0) + 1.0)
+    rows_in = jnp.concatenate([m1_v[q, 16:24, :] for q in range(NT)], axis=0)
+    rows_wide = jnp.concatenate([rows_in] * DGROUPS, axis=1)
+    row_tile = (iota((LANES, DOC_TILES * BLOCK), 1) // BLOCK).astype(F32)
+    same_row = jnp.where(rows_wide == row_tile, 1.0, 0.0)
+    arrived(3, rsr_v, NT)
+    rst_v[...] = jnp.concatenate([rsr_v[q] for q in range(NT)], axis=0).T
+    my_rows = rst_v[pl.ds(pl.multiple_of(TX * lax.rem(j, 4), TX), TX), :]
+    row_scale = lax.rsqrt(dot(my_rows, same_row, NN) + 1.0)
     row_square = row_scale * row_scale
 
     arrived(4, trecv.at[1], NT)
@@ -316,10 +351,9 @@
     to_terms(5, lambda q: tsend.at[2, q], trecv.at[2])
     f0 = stacked(image * row_scale, DGROUPS)
     rest, last = all_sum(0, 6, packed(fold(dot(f0, f0, TN)) * (1.0 / N_DOCS), None))
-    for g in range(DGROUPS):
-        f0_v[g] = f0[g * TX : (g + 1) * TX]
-    trecv[4, j] = f0_v[j // 4]
-    to_terms(8, lambda q: f0_v.at[q // 4], trecv.at[4])
+    pack(f0, pk_v.at[0])
+    pkr_v[0, j] = pk_v[0, j]
+    to_terms(8, lambda q: pk_v.at[0, q], pkr_v.at[0])
 
     for q in range(ND):
         hit = iota((TERM_TILES * BLOCK, LANES), 0).astype(F32) == d1_v[q, 8:9, :]
@@ -369,10 +403,10 @@
     drecv[2, i] = share_v[i, 0:DX, :]
     to_docs(13, lambda q: share_v.at[q, pl.ds(0, DX), :], drecv.at[2])
 
+    rest()
     arrived(10, drecv.at[1], ND)
     pieces = jnp.concatenate([drecv[1, q] for q in range(ND)], axis=0)
     term_exchange(14, 3, forward_product(split(pieces)))
-    rest()
     z = last()
     r1 = unpacked(z, 2)
     pad = jnp.zeros((LANES - BLOCK, LANES), F32)
@@ -390,10 +424,9 @@
     x2 = dot(stacked(image, DGROUPS), k21, NTR) - expected
     t3 = dot(x2, jnp.concatenate([x2, u1], axis=1), TN) * (1.0 / N_DOCS)
     rest, last = all_sum(2, 15, packed(fold(t3[:, :LANES]), fold(t3[:, LANES:])))
-    for g in range(DGROUPS):
-        x2_v[g] = x2[g * TX : (g + 1) * TX]
-    trecv[5, j] = x2_v[j // 4]
-    to_terms(17, lambda q: x2_v.at[q // 4], trecv.at[5])
+    pack(x2, pk_v.at[1])
+    pkr_v[1, j] = pk_v[1, j]
+    to_terms(17, lambda q: pk_v.at[1, q], pkr_v.at[1])
     arrived(13, drecv.at[2], ND)
     right_x = jnp.concatenate([drecv[2, q] for q in range(ND)], axis=0)
     rest()
@@ -406,10 +439,10 @@
     coef_o[0] = transposed(upper1)[:, :BLOCK]
     coef_o[1] = (p0 + r1)[:, :BLOCK]
     coef_o[2] = transposed(upper2)[:, :BLOCK]
-    arrived(8, trecv.at[4], NT)
-    left_u = dot(jnp.concatenate([trecv[4, q] for q in range(NT)], axis=0), k1, NTR)
-    arrived(17, trecv.at[5], NT)
-    left_x = jnp.concatenate([trecv[5, q] for q in range(NT)], axis=0)
+    arrived(8, pkr_v.at[0], NT)
+    left_u = dot(unpack(pkr_v.at[0]), k1, NTR)
+    arrived(17, pkr_v.at[1], NT)
+    left_x = unpack(pkr_v.at[1])
 
     z = last()
     r2 = unpacked(z, 2)
@@ -419,7 +452,7 @@
     rep = inverse3 + roll(inverse3, 16)
     rep = rep + roll(rep, 32)
     rep = rep + roll(rep, 64)
-    mine = iota((2 * BLOCK, LANES), 1) // BLOCK == iota((2 * BLOCK, LANES), 0) // BLOCK + 2 * lax.rem(j, 4)
+    mine = iota((2 * BLOCK, LANES), 1) // BLOCK == iota((2 * BLOCK, LANES), 0) // BLOCK
     left = dot(jnp.where(mine, jnp.concatenate([rep, rep], axis=0), 0.0), left_x, NTR)
     left_o[:, 0:TILE] = left[0:BLOCK]
     left_o[:, TILE : 2 * TILE] = left[BLOCK : 2 * BLOCK]
@@ -456,11 +489,11 @@
             pltpu.VMEM((TERM_TILES, BLOCK, TILE), F32),
             pltpu.VMEM((DOC_TILES * BLOCK, NT * LANES), BF16),
             pltpu.VMEM((TERM_TILES * BLOCK, ND * LANES), BF16),
-            pltpu.VMEM((NT, 16, LANES), F32),
+            pltpu.VMEM((NT, 24, LANES), F32),
             pltpu.VMEM((ND, 16, LANES), F32),
             pltpu.VMEM((ND, SLOTS, TILE), F32),
             pltpu.VMEM((4, NT, TX, LANES), F32),
-            pltpu.VMEM((6, NT, TX, LANES), F32),
+            pltpu.VMEM((4, NT, TX, LANES), F32),
             pltpu.VMEM((2, ND, DX, LANES), F32),
             pltpu.VMEM((3, ND, DX, LANES), F32),
             pltpu.VMEM((3, ND, 8, LANES), F32),
@@ -468,14 +501,17 @@
             pltpu.VMEM((TILE, LANES), F32),
             pltpu.VMEM((TGROUPS, LANES, LANES), F32),
             pltpu.VMEM((TILE, ND * SLOTS), F32),
-            pltpu.VMEM((DGROUPS, TX, LANES), F32),
-            pltpu.VMEM((DGROUPS, TX, LANES), F32),
+            pltpu.VMEM((DGROUPS, SLOTS, LANES), F32),
+            pltpu.VMEM((NT, SLOTS, LANES), F32),
+            pltpu.VMEM((LANES, LANES), F32),
+            pltpu.VMEM((2, NT, 8, LANES), F32),
+            pltpu.VMEM((2, NT, 8, LANES), F32),
             pltpu.SemaphoreType.DMA((SLOTS + 4,)),
             pltpu.SemaphoreType.DMA((18,)),
             pltpu.SemaphoreType.DMA((18,)),
         ],
         compiler_params=pltpu.CompilerParams(
-            collective_id=0, has_side_effects=True, vmem_limit_bytes=65000000
+            collective_id=0, has_side_effects=True, vmem_limit_bytes=56000000
         ),
     )(
         counts,

time: 82 us -> 77.3 us (0.943)
  Pallas kernels: 77.9 us -> 74.5 us
  local copies, waits for them, and re-layouts: 2.56 us -> 1.3 us
    pallas_call x1, Pallas kernels: 77.1 us -> 73.8 us  [on_device(): pl.pallas_call(kernel, out_shape=shapes, in_specs=[anywhere] * 5, out_spe...]
    unnamed x6 -> x4, local copies, waits for them, and re-layouts: 2.56 us -> 1.3 us
where the time goes in v3:
time: 77.3 us; the launch traced here: 77.1 us
  Pallas kernels  74.5 us (96%)
  local copies, waits for them, and re-layouts  1.3 us (2%)
  between operations  1.3 us (2%)
    pallas_call x1, Pallas kernels, on_device(): pl.pallas_call(kernel, out_shape=shapes, in_specs=[anywhere] * 5, out_spe...  73.8 us

profile of v3, /device:TPU:1, one launch (start us, length us, event | category | flops | bytes accessed | tf_op | source)
XLA Modules:
  0.0 77.1 jit_solution(14398205676448957132)
XLA Ops:
  1.3 0.0 copy-start
  1.3 0.6 copy-done
  1.9 0.0 copy-start.1
  1.9 0.7 copy-done.1
  2.6 73.8 %shard_map.76 = (f32[16,1024]{1,0:T(8,128)S(1)}, f32[16,4096]{1,0:T(8,128)S(1)}, f32[5,16,16]{2,1,0:T(8,128)S(1)}) custom-call(s32[1,1]{1,0:T(1,128)S(6)} %copy.8.cnt_h, s32[1,8]{1,0:T(1,128)S(1)} %bitcast.3, s32[1,8]{1,0:T(1,128)S(1)} %bitcast.4, bf16[8,512,512]{2,1,0:T(8,128)(2,1)} %bitcast.5, f32[16,32768]{1,0:T(8,128)} %start_h.1), custom_call_target="tpu_custom_call" | custom-call | tf_op jit(solution)/shard_map/pallas_call | solution.py:479
  76.4 0.8 shard_map.77
Async XLA Ops:
  1.3 0.7 copy-start
  1.9 0.7 copy-start.1

commit v4 on v3

--- a/solution.py
+++ b/solution.py
@@ -44,12 +44,6 @@
     return jnp.concatenate([hi, lo], axis=0)
 
 
-def by_onehot(x, onehot, contract):
-    n = x.shape[0]
-    both = dot(halves(x), onehot, contract, None)
-    return both[:n] + both[n:]
-
-
 def iota(shape, dim):
     return lax.broadcasted_iota(jnp.int32, shape, dim)
 
@@ -153,7 +147,7 @@
             q = lax.rem(j + d, NT)
             pltpu.make_async_remote_copy(
                 src_ref=src_of(q), dst_ref=dst.at[j],
-                send_sem=send_sem.at[n], recv_sem=recv_sem.at[n],
+                send_sem=send_sem.at[n], recv_sem=recv_sem.at[n, 0],
                 device_id=(i, q), device_id_type=MESH,
             ).start()
             return carry
@@ -165,40 +159,108 @@
             q = lax.rem(i + d, ND)
             pltpu.make_async_remote_copy(
                 src_ref=src_of(q), dst_ref=dst.at[i],
-                send_sem=send_sem.at[n], recv_sem=recv_sem.at[n],
+                send_sem=send_sem.at[n], recv_sem=recv_sem.at[n, 0],
                 device_id=(q, j), device_id_type=MESH,
             ).start()
             return carry
         lax.fori_loop(1, ND, send, 0)
         pending.append((n, dst.at[pl.ds(0, ND - 1)]))
 
-    def arrived(n, dst, peers):
+    def arrived(n, dst, peers, group=0):
         part = dst.at[pl.ds(0, peers - 1)]
-        pltpu.make_async_copy(part, part, recv_sem.at[n]).wait()
-
-    def term_exchange(n, slot, total):
-        for q in range(NT):
-            tsend[slot, q] = total[q * TX : (q + 1) * TX]
-        trecv[slot, j] = tsend[slot, j]
-        to_terms(n, lambda q: tsend.at[slot, q], trecv.at[slot])
-
-    def doc_exchange(n, slot, total):
-        for q in range(ND):
-            dsend[slot, q] = total[q * DX : (q + 1) * DX]
-        drecv[slot, i] = dsend[slot, i]
-        to_docs(n, lambda q: dsend.at[slot, q], drecv.at[slot])
-
-    def forward_product(x):
+        pltpu.make_async_copy(part, part, recv_sem.at[n, group]).wait()
+
+    y = j // 4
+    t0 = lax.rem(j, 4)
+    xl = i // 4
+    z0 = lax.rem(i, 4)
+
+    def term_block_send(n, slot, block, dy):
+        yb = lax.rem(y + dy, 4)
+        tsend[slot, pl.ds(4 * yb, 4)] = block.reshape(4, TX, LANES)
+        if dy == 0:
+            trecv[slot, j] = tsend[slot, j]
+            pending.append((n, trecv.at[slot, pl.ds(0, NT - 1)]))
+        for t in (2, 3, 1) if dy == 0 else (2, 3, 1, 0):
+            q = 4 * yb + lax.rem(t0 + t, 4)
+            pltpu.make_async_remote_copy(
+                src_ref=tsend.at[slot, q], dst_ref=trecv.at[slot, j],
+                send_sem=send_sem.at[n], recv_sem=recv_sem.at[n, 1 if dy == 2 else 0],
+                device_id=(i, q), device_id_type=MESH,
+            ).start()
+
+    def doc_block_send(n, slot, block, dx):
+        xb = lax.rem(xl + dx, 2)
+        dsend[slot, pl.ds(4 * xb, 4)] = block.reshape(4, DX, LANES)
+        if dx == 0:
+            drecv[slot, i] = dsend[slot, i]
+            pending.append((n, drecv.at[slot, pl.ds(0, ND - 1)]))
+        for t in (2, 1, 3) if dx == 0 else (2, 1, 3, 0):
+            q = 4 * xb + lax.rem(z0 + t, 4)
+            pltpu.make_async_remote_copy(
+                src_ref=dsend.at[slot, q], dst_ref=drecv.at[slot, i],
+                send_sem=send_sem.at[n], recv_sem=recv_sem.at[n, dx],
+                device_id=(q, j), device_id_type=MESH,
+            ).start()
+
+    def forward_exchange(n, slot, x):
         lane_slot = iota((TILE, LANES), 1) // BLOCK
-        total = None
+        weights = []
         for k in range(SLOTS):
             masked = [jnp.where(lane_slot == k, part, 0.0).astype(BF16) for part in x]
-            weights = masked[0] if len(masked) == 1 else jnp.concatenate(masked, axis=1)
-            part = dot(tiles_v[k], weights, NN, None)
-            total = part if total is None else total + part
-        if len(x) == 2:
-            total = total[:, :LANES] + total[:, LANES:]
-        return total
+            weights.append(masked[0] if len(masked) == 1 else jnp.concatenate(masked, axis=1))
+        for pair in ((2, 1), (3, 0)):
+            rows = [pl.ds(pl.multiple_of(128 * lax.rem(y + dy, 4), 128), 128) for dy in pair]
+            total = None
+            for k in range(SLOTS):
+                lhs = jnp.concatenate([tiles_v[k, r, :] for r in rows], axis=0)
+                part = dot(lhs, weights[k], NN, None)
+                total = part if total is None else total + part
+            if len(x) == 2:
+                total = total[:, :LANES] + total[:, LANES:]
+            term_block_send(n, slot, total[:128], pair[0])
+            term_block_send(n, slot, total[128:], pair[1])
+
+    def term_sum(n, slot):
+        acc = None
+        for rel in (0, 1, 3, 2):
+            if rel == 0:
+                arrived(n, trecv.at[slot], 12)
+            if rel == 2:
+                arrived(n, trecv.at[slot], 5, 1)
+            yb = lax.rem(y + rel, 4)
+            block = trecv[slot, pl.ds(4 * yb, 4)]
+            flat = jnp.concatenate([block[t] for t in range(4)], axis=1)
+            onehot = st_v[:, pl.ds(pl.multiple_of(512 * yb, 512), 512)]
+            part = dot(halves(flat), onehot, NTR, None)
+            acc = part if acc is None else acc + part
+        return acc[:TX] + acc[TX:]
+
+    def term_gather(n, slot, x):
+        both = halves(x)
+        for dy in (2, 1, 3, 0):
+            yb = lax.rem(y + dy, 4)
+            part = dot(both, st_v[:, pl.ds(pl.multiple_of(512 * yb, 512), 512)], NN, None)
+            term_block_send(n, slot, stacked(part[:TX] + part[TX:], 4), dy)
+
+    def doc_sum(n, slot):
+        acc = None
+        for dx in (0, 1):
+            arrived(n, drecv.at[slot], 4 + dx, dx)
+            xb = lax.rem(xl + dx, 2)
+            block = drecv[slot, pl.ds(4 * xb, 4)]
+            flat = jnp.concatenate([block[t] for t in range(4)], axis=1)
+            onehot = sd_v[:, pl.ds(pl.multiple_of(512 * xb, 512), 512)]
+            part = dot(halves(flat), onehot, NTR, None)
+            acc = part if acc is None else acc + part
+        return acc[:DX] + acc[DX:]
+
+    def doc_gather(n, slot, x):
+        both = halves(x)
+        for dx in (1, 0):
+            xb = lax.rem(xl + dx, 2)
+            part = dot(both, sd_v[:, pl.ds(pl.multiple_of(512 * xb, 512), 512)], NN, None)
+            doc_block_send(n, slot, stacked(part[:DX] + part[DX:], 4), dx)
 
     def split(x):
         hi = x.astype(BF16).astype(F32)
@@ -229,10 +291,6 @@
             for h in range(4):
                 rows.append(ref[q] if h == 0 else roll(ref[q], LANES - 32 * h))
         return jnp.concatenate(rows, axis=0)
-
-    def term_sum(slot):
-        flat = jnp.concatenate([trecv[slot, q] for q in range(NT)], axis=1)
-        return by_onehot(flat, st_v[...], NTR)
 
     def all_sum(n, base, z):
         za[n, i] = z
@@ -327,7 +385,7 @@
         gram = gram + m1_v[q, 0:8, :]
     _, inverse0 = factor(unpacked(gram, 0))
     k0 = spread(inverse0)
-    term_exchange(4, 1, forward_product([dot(scaled_slots, k0, NTR)]))
+    forward_exchange(4, 1, [dot(scaled_slots, k0, NTR)])
 
     for q in range(NT):
         hit = iota((DOC_TILES * BLOCK, LANES), 0).astype(F32) == m1_v[q, 8:9, :]
@@ -342,13 +400,8 @@
     row_scale = lax.rsqrt(dot(my_rows, same_row, NN) + 1.0)
     row_square = row_scale * row_scale
 
-    arrived(4, trecv.at[1], NT)
-    image = term_sum(1)
-    wide = by_onehot(image * row_square, st_v[...], NN)
-    for q in range(NT):
-        tsend[2, q] = wide[:, q * LANES : (q + 1) * LANES]
-    trecv[2, j] = tsend[2, j]
-    to_terms(5, lambda q: tsend.at[2, q], trecv.at[2])
+    image = term_sum(4, 1)
+    term_gather(5, 2, image * row_square)
     f0 = stacked(image * row_scale, DGROUPS)
     rest, last = all_sum(0, 6, packed(fold(dot(f0, f0, TN)) * (1.0 / N_DOCS), None))
     pack(f0, pk_v.at[0])
@@ -359,16 +412,22 @@
         hit = iota((TERM_TILES * BLOCK, LANES), 0).astype(F32) == d1_v[q, 8:9, :]
         sd_v[:, q * LANES : (q + 1) * LANES] = jnp.where(hit, 1.0, 0.0).astype(BF16)
     rest()
-    arrived(5, trecv.at[2], NT)
+    arrived(5, trecv.at[2], 12)
+    arrived(5, trecv.at[2], 5, 1)
     pieces = jnp.concatenate([trecv[2, q] for q in range(NT)], axis=0).T
     hi = pieces.astype(BF16)
     lo = (pieces - hi.astype(F32)).astype(BF16)
-    back = []
+    pairs = []
     for k in range(SLOTS):
-        cut = slice(k * BLOCK, (k + 1) * BLOCK)
-        both = dot(jnp.concatenate([hi[cut], lo[cut]], axis=0), tiles_v[k], NN, None)
-        back.append(both[:BLOCK] + both[BLOCK:])
-    doc_exchange(9, 0, jnp.concatenate(back, axis=0).T)
+        part = slice(k * BLOCK, (k + 1) * BLOCK)
+        pairs.append(jnp.concatenate([hi[part], lo[part]], axis=0))
+    for dx in (1, 0):
+        columns = pl.ds(pl.multiple_of(256 * lax.rem(xl + dx, 2), 256), 256)
+        back = []
+        for k in range(SLOTS):
+            both = dot(pairs[k], tiles_v[k, :, columns], NN, None)
+            back.append(both[:BLOCK] + both[BLOCK:])
+        doc_block_send(9, 0, jnp.concatenate(back, axis=0).T, dx)
 
     cols_wide = jnp.concatenate([cols_in] * TGROUPS, axis=1)
     tile_at = (iota((ND * SLOTS, TERM_TILES * BLOCK), 1) // BLOCK).astype(F32)
@@ -387,14 +446,8 @@
     expected = dot(e_share, spread(p0), NTR)
     u1 = dot(f0, k1, NTR)
 
-    arrived(9, drecv.at[0], ND)
-    flat = jnp.concatenate([drecv[0, q] for q in range(ND)], axis=1)
-    image = by_onehot(flat, sd_v[...], NTR)
-    wide = by_onehot(image * col_square, sd_v[...], NN)
-    for q in range(ND):
-        dsend[1, q] = wide[:, q * LANES : (q + 1) * LANES]
-    drecv[1, i] = dsend[1, i]
-    to_docs(10, lambda q: dsend.at[1, q], drecv.at[1])
+    image = doc_sum(9, 0)
+    doc_gather(10, 1, image * col_square)
     b1 = dot(stacked(image * col_share, TGROUPS), k1, NTR) - expected
     t2 = dot(b1, jnp.concatenate([b1, e_share], axis=1), TN) * (1.0 / N_TERMS)
     rest, last = all_sum(1, 11, packed(fold(t2[:, :LANES]), fold(t2[:, LANES:])))
@@ -404,9 +457,10 @@
     to_docs(13, lambda q: share_v.at[q, pl.ds(0, DX), :], drecv.at[2])
 
     rest()
-    arrived(10, drecv.at[1], ND)
+    arrived(10, drecv.at[1], 4)
+    arrived(10, drecv.at[1], 5, 1)
     pieces = jnp.concatenate([drecv[1, q] for q in range(ND)], axis=0)
-    term_exchange(14, 3, forward_product(split(pieces)))
+    forward_exchange(14, 3, split(pieces))
     z = last()
     r1 = unpacked(z, 2)
     pad = jnp.zeros((LANES - BLOCK, LANES), F32)
@@ -419,8 +473,7 @@
     known = dot(k2, spread(p0 + r1), NN) + dot(spread(p02), k1, NN)
     expected = dot(f0, known, NTR)
 
-    arrived(14, trecv.at[3], NT)
-    image = term_sum(3) * row_scale
+    image = term_sum(14, 3) * row_scale
     x2 = dot(stacked(image, DGROUPS), k21, NTR) - expected
     t3 = dot(x2, jnp.concatenate([x2, u1], axis=1), TN) * (1.0 / N_DOCS)
     rest, last = all_sum(2, 15, packed(fold(t3[:, :LANES]), fold(t3[:, LANES:])))
@@ -508,7 +561,7 @@
             pltpu.VMEM((2, NT, 8, LANES), F32),
             pltpu.SemaphoreType.DMA((SLOTS + 4,)),
             pltpu.SemaphoreType.DMA((18,)),
-            pltpu.SemaphoreType.DMA((18,)),
+            pltpu.SemaphoreType.DMA((18, 2)),
         ],
         compiler_params=pltpu.CompilerParams(
             collective_id=0, has_side_effects=True, vmem_limit_bytes=56000000

time: 77.3 us -> 73.8 us (0.955)
  Pallas kernels: 74.5 us -> 71 us
    pallas_call x1, Pallas kernels: 73.8 us -> 70.3 us  [on_device(): pl.pallas_call(kernel, out_shape=shapes, in_specs=[anywhere] * 5, out_spe...]
where the time goes in v4:
time: 73.8 us; the launch traced here: 73.6 us
  Pallas kernels  71 us (96%)
  local copies, waits for them, and re-layouts  1.3 us (2%)
  between operations  1.3 us (2%)
    pallas_call x1, Pallas kernels, on_device(): pl.pallas_call(kernel, out_shape=shapes, in_specs=[anywhere] * 5, out_spe...  70.3 us

profile of v4, /device:TPU:1, one launch (start us, length us, event | category | flops | bytes accessed | tf_op | source)
XLA Modules:
  0.0 73.6 jit_solution(6469956648268518344)
XLA Ops:
  1.3 0.0 copy-start
  1.3 0.6 copy-done
  1.9 0.0 copy-start.1
  1.9 0.7 copy-done.1
  2.6 70.3 %shard_map.76 = (f32[16,1024]{1,0:T(8,128)S(1)}, f32[16,4096]{1,0:T(8,128)S(1)}, f32[5,16,16]{2,1,0:T(8,128)S(1)}) custom-call(s32[1,1]{1,0:T(1,128)S(6)} %copy.8.cnt_h, s32[1,8]{1,0:T(1,128)S(1)} %bitcast.3, s32[1,8]{1,0:T(1,128)S(1)} %bitcast.4, bf16[8,512,512]{2,1,0:T(8,128)(2,1)} %bitcast.5, f32[16,32768]{1,0:T(8,128)} %start_h.1), custom_call_target="tpu_custom_call" | custom-call | tf_op jit(solution)/shard_map/pallas_call | solution.py:532
  72.9 0.8 %shard_map.77 = (f32[16,1024]{1,0:T(8,128)}, f32[16,4096]{1,0:T(8,128)}, f32[5,16,16]{2,1,0:T(8,128)}) custom-call(f32[16,1024]{1,0:T(8,128)S(1)} %get-tuple-element.6.left_i, f32[16,4096]{1,0:T(8,128)S(1)} %get-tuple-element.7.right_i, f32[5,16,16]{2,1,0:T(8,128)S(1)} %get-tuple-element.8.coef_i), custom_call_target="tpu_custom_call" | custom-call | tf_op jit(solution)/shard_map/pallas_call | solution.py:576
Async XLA Ops:
  1.3 0.7 copy-start
  1.9 0.7 copy-start.1

commit v5 on v4

--- a/solution.py
+++ b/solution.py
@@ -175,33 +175,49 @@
     xl = i // 4
     z0 = lax.rem(i, 4)
 
-    def term_block_send(n, slot, block, dy):
+    def term_block_send(n, slot, block, dy, looped=False):
         yb = lax.rem(y + dy, 4)
         tsend[slot, pl.ds(4 * yb, 4)] = block.reshape(4, TX, LANES)
         if dy == 0:
             trecv[slot, j] = tsend[slot, j]
             pending.append((n, trecv.at[slot, pl.ds(0, NT - 1)]))
-        for t in (2, 3, 1) if dy == 0 else (2, 3, 1, 0):
+
+        def send(t, carry=0):
             q = 4 * yb + lax.rem(t0 + t, 4)
             pltpu.make_async_remote_copy(
                 src_ref=tsend.at[slot, q], dst_ref=trecv.at[slot, j],
                 send_sem=send_sem.at[n], recv_sem=recv_sem.at[n, 1 if dy == 2 else 0],
                 device_id=(i, q), device_id_type=MESH,
             ).start()
-
-    def doc_block_send(n, slot, block, dx):
+            return carry
+
+        if looped:
+            lax.fori_loop(1, 4 if dy == 0 else 5, send, 0)
+        else:
+            for t in (2, 3, 1) if dy == 0 else (2, 3, 1, 0):
+                send(t)
+
+    def doc_block_send(n, slot, block, dx, looped=False):
         xb = lax.rem(xl + dx, 2)
         dsend[slot, pl.ds(4 * xb, 4)] = block.reshape(4, DX, LANES)
         if dx == 0:
             drecv[slot, i] = dsend[slot, i]
             pending.append((n, drecv.at[slot, pl.ds(0, ND - 1)]))
-        for t in (2, 1, 3) if dx == 0 else (2, 1, 3, 0):
+
+        def send(t, carry=0):
             q = 4 * xb + lax.rem(z0 + t, 4)
             pltpu.make_async_remote_copy(
                 src_ref=dsend.at[slot, q], dst_ref=drecv.at[slot, i],
                 send_sem=send_sem.at[n], recv_sem=recv_sem.at[n, dx],
                 device_id=(q, j), device_id_type=MESH,
             ).start()
+            return carry
+
+        if looped:
+            lax.fori_loop(1, 4 if dx == 0 else 5, send, 0)
+        else:
+            for t in (2, 1, 3) if dx == 0 else (2, 1, 3, 0):
+                send(t)
 
     def forward_exchange(n, slot, x):
         lane_slot = iota((TILE, LANES), 1) // BLOCK
@@ -241,7 +257,7 @@
         for dy in (2, 1, 3, 0):
             yb = lax.rem(y + dy, 4)
             part = dot(both, st_v[:, pl.ds(pl.multiple_of(512 * yb, 512), 512)], NN, None)
-            term_block_send(n, slot, stacked(part[:TX] + part[TX:], 4), dy)
+            term_block_send(n, slot, stacked(part[:TX] + part[TX:], 4), dy, dy in (0, 2))
 
     def doc_sum(n, slot):
         acc = None
@@ -260,7 +276,7 @@
         for dx in (1, 0):
             xb = lax.rem(xl + dx, 2)
             part = dot(both, sd_v[:, pl.ds(pl.multiple_of(512 * xb, 512), 512)], NN, None)
-            doc_block_send(n, slot, stacked(part[:DX] + part[DX:], 4), dx)
+            doc_block_send(n, slot, stacked(part[:DX] + part[DX:], 4), dx, True)
 
     def split(x):
         hi = x.astype(BF16).astype(F32)
@@ -454,13 +470,13 @@
     for g in range(TGROUPS):
         share_v[g, 0:DX, :] = b1[g * DX : (g + 1) * DX]
     drecv[2, i] = share_v[i, 0:DX, :]
-    to_docs(13, lambda q: share_v.at[q, pl.ds(0, DX), :], drecv.at[2])
 
     rest()
     arrived(10, drecv.at[1], 4)
     arrived(10, drecv.at[1], 5, 1)
     pieces = jnp.concatenate([drecv[1, q] for q in range(ND)], axis=0)
     forward_exchange(14, 3, split(pieces))
+    to_docs(13, lambda q: share_v.at[q, pl.ds(0, DX), :], drecv.at[2])
     z = last()
     r1 = unpacked(z, 2)
     pad = jnp.zeros((LANES - BLOCK, LANES), F32)
@@ -480,9 +496,9 @@
     pack(x2, pk_v.at[1])
     pkr_v[1, j] = pk_v[1, j]
     to_terms(17, lambda q: pk_v.at[1, q], pkr_v.at[1])
+    rest()
     arrived(13, drecv.at[2], ND)
     right_x = jnp.concatenate([drecv[2, q] for q in range(ND)], axis=0)
-    rest()
 
     start_st = start_v[pl.ds(i * 8, 8)].reshape(LANES, TILE)
     k20 = dot(k2, dot(kr1, k0, NN), NN)

time: 73.8 us -> 73.2 us (level)
  no operation moved by 1% of the time
where the time goes in v5:
time: 73.2 us; the launch traced here: 73 us
  Pallas kernels  70.4 us (96%)
  local copies, waits for them, and re-layouts  1.3 us (2%)
  between operations  1.3 us (2%)
    pallas_call x1, Pallas kernels, on_device(): pl.pallas_call(kernel, out_shape=shapes, in_specs=[anywhere] * 5, out_spe...  69.7 us

profile of v5, /device:TPU:1, one launch (start us, length us, event | category | flops | bytes accessed | tf_op | source)
XLA Modules:
  0.0 73.0 jit_solution(406641930110775800)
XLA Ops:
  1.3 0.0 copy-start
  1.3 0.6 copy-done
  1.9 0.0 copy-start.1
  1.9 0.7 copy-done.1
  2.6 69.7 %shard_map.76 = (f32[16,1024]{1,0:T(8,128)S(1)}, f32[16,4096]{1,0:T(8,128)S(1)}, f32[5,16,16]{2,1,0:T(8,128)S(1)}) custom-call(s32[1,1]{1,0:T(1,128)S(6)} %copy.8.cnt_h, s32[1,8]{1,0:T(1,128)S(1)} %bitcast.3, s32[1,8]{1,0:T(1,128)S(1)} %bitcast.4, bf16[8,512,512]{2,1,0:T(8,128)(2,1)} %bitcast.5, f32[16,32768]{1,0:T(8,128)} %start_h.1), custom_call_target="tpu_custom_call" | custom-call | tf_op jit(solution)/shard_map/pallas_call | solution.py:548
  72.3 0.8 %shard_map.77 = (f32[16,1024]{1,0:T(8,128)}, f32[16,4096]{1,0:T(8,128)}, f32[5,16,16]{2,1,0:T(8,128)}) custom-call(f32[16,1024]{1,0:T(8,128)S(1)} %get-tuple-element.6.left_i, f32[16,4096]{1,0:T(8,128)S(1)} %get-tuple-element.7.right_i, f32[5,16,16]{2,1,0:T(8,128)S(1)} %get-tuple-element.8.coef_i), custom_call_target="tpu_custom_call" | custom-call | tf_op jit(solution)/shard_map/pallas_call | solution.py:592
Async XLA Ops:
  1.3 0.7 copy-start
  1.9 0.7 copy-start.1

commit v6 on v5

--- a/solution.py
+++ b/solution.py
@@ -372,9 +372,9 @@
     cs_v[i] = col_sums[:SLOTS]
 
     pl.semaphore_wait(bar, ND - 1 + NT - 1)
+    to_terms(2, lambda q: m1_v.at[j], m1_v)
     to_docs(0, lambda q: d1_v.at[i], d1_v)
     to_docs(1, lambda q: cs_v.at[i], cs_v)
-    to_terms(2, lambda q: m1_v.at[j], m1_v)
 
     row_sums = jnp.zeros((16, TILE), F32)
     for k in range(SLOTS):
@@ -389,13 +389,13 @@
 
     arrived(0, d1_v, ND)
     arrived(1, cs_v, ND)
+    arrived(2, m1_v, NT)
     cols_in = jnp.concatenate([d1_v[q, 0:8, :] for q in range(ND)], axis=0)
     sums_t = jnp.concatenate([cs_v[q] for q in range(ND)], axis=0).T
     cst_v[...] = sums_t
     same_col = jnp.where(cols_in == my_col[0:1, :], 1.0, 0.0)
     col_scale = lax.rsqrt(dot(sums_t, same_col, NN) + 1.0)
     scaled_slots = slots_v[...] * col_scale
-    arrived(2, m1_v, NT)
     gram = m1_v[0, 0:8, :]
     for q in range(1, NT):
         gram = gram + m1_v[q, 0:8, :]

time: 73.2 us -> 71.3 us (0.974)
  Pallas kernels: 70.4 us -> 68.5 us
    pallas_call x1, Pallas kernels: 69.7 us -> 67.8 us  [on_device(): pl.pallas_call(kernel, out_shape=shapes, in_specs=[anywhere] * 5, out_spe...]
where the time goes in v6:
time: 71.3 us; the launch traced here: 71.1 us
  Pallas kernels  68.5 us (96%)
  local copies, waits for them, and re-layouts  1.3 us (2%)
  between operations  1.3 us (2%)
    pallas_call x1, Pallas kernels, on_device(): pl.pallas_call(kernel, out_shape=shapes, in_specs=[anywhere] * 5, out_spe...  67.8 us

profile of v6, /device:TPU:1, one launch (start us, length us, event | category | flops | bytes accessed | tf_op | source)
XLA Modules:
  0.0 71.1 jit_solution(10670542132335561863)
XLA Ops:
  1.3 0.0 copy-start
  1.3 0.6 copy-done
  1.9 0.0 copy-start.1
  1.9 0.7 copy-done.1
  2.6 67.8 %shard_map.76 = (f32[16,1024]{1,0:T(8,128)S(1)}, f32[16,4096]{1,0:T(8,128)S(1)}, f32[5,16,16]{2,1,0:T(8,128)S(1)}) custom-call(s32[1,1]{1,0:T(1,128)S(6)} %copy.8.cnt_h, s32[1,8]{1,0:T(1,128)S(1)} %bitcast.3, s32[1,8]{1,0:T(1,128)S(1)} %bitcast.4, bf16[8,512,512]{2,1,0:T(8,128)(2,1)} %bitcast.5, f32[16,32768]{1,0:T(8,128)} %start_h.1), custom_call_target="tpu_custom_call" | custom-call | tf_op jit(solution)/shard_map/pallas_call | solution.py:548
  70.4 0.8 %shard_map.77 = (f32[16,1024]{1,0:T(8,128)}, f32[16,4096]{1,0:T(8,128)}, f32[5,16,16]{2,1,0:T(8,128)}) custom-call(f32[16,1024]{1,0:T(8,128)S(1)} %get-tuple-element.6.left_i, f32[16,4096]{1,0:T(8,128)S(1)} %get-tuple-element.7.right_i, f32[5,16,16]{2,1,0:T(8,128)S(1)} %get-tuple-element.8.coef_i), custom_call_target="tpu_custom_call" | custom-call | tf_op jit(solution)/shard_map/pallas_call | solution.py:592
Async XLA Ops:
  1.3 0.7 copy-start
  1.9 0.7 copy-start.1

commit v7 on v6

--- a/solution.py
+++ b/solution.py
@@ -144,7 +144,7 @@
 
     def to_terms(n, src_of, dst):
         def send(d, carry):
-            q = lax.rem(j + d, NT)
+            q = lax.rem(j + lax.rem(d + 6, NT - 1) + 1, NT)
             pltpu.make_async_remote_copy(
                 src_ref=src_of(q), dst_ref=dst.at[j],
                 send_sem=send_sem.at[n], recv_sem=recv_sem.at[n, 0],
@@ -156,7 +156,7 @@
 
     def to_docs(n, src_of, dst):
         def send(d, carry):
-            q = lax.rem(i + d, ND)
+            q = lax.rem(i + lax.rem(d + 2, ND - 1) + 1, ND)
             pltpu.make_async_remote_copy(
                 src_ref=src_of(q), dst_ref=dst.at[i],
                 send_sem=send_sem.at[n], recv_sem=recv_sem.at[n, 0],

time: 71.3 us -> 72.4 us (1.015)
  Pallas kernels: 68.5 us -> 69.7 us
    pallas_call x1, Pallas kernels: 67.8 us -> 68.9 us  [on_device(): pl.pallas_call(kernel, out_shape=shapes, in_specs=[anywhere] * 5, out_spe...]
where the time goes in v7:
time: 72.4 us; the launch traced here: 72.3 us
  Pallas kernels  69.7 us (96%)
  local copies, waits for them, and re-layouts  1.3 us (2%)
  between operations  1.3 us (2%)
    pallas_call x1, Pallas kernels, on_device(): pl.pallas_call(kernel, out_shape=shapes, in_specs=[anywhere] * 5, out_spe...  68.9 us

profile of v7, /device:TPU:1, one launch (start us, length us, event | category | flops | bytes accessed | tf_op | source)
XLA Modules:
  0.0 72.3 jit_solution(13352528915197812499)
XLA Ops:
  1.3 0.0 copy-start
  1.3 0.6 copy-done
  1.9 0.0 copy-start.1
  1.9 0.7 copy-done.1
  2.6 68.9 %shard_map.76 = (f32[16,1024]{1,0:T(8,128)S(1)}, f32[16,4096]{1,0:T(8,128)S(1)}, f32[5,16,16]{2,1,0:T(8,128)S(1)}) custom-call(s32[1,1]{1,0:T(1,128)S(6)} %copy.8.cnt_h, s32[1,8]{1,0:T(1,128)S(1)} %bitcast.3, s32[1,8]{1,0:T(1,128)S(1)} %bitcast.4, bf16[8,512,512]{2,1,0:T(8,128)(2,1)} %bitcast.5, f32[16,32768]{1,0:T(8,128)} %start_h.1), custom_call_target="tpu_custom_call" | custom-call | tf_op jit(solution)/shard_map/pallas_call | solution.py:548
  71.5 0.8 %shard_map.77 = (f32[16,1024]{1,0:T(8,128)}, f32[16,4096]{1,0:T(8,128)}, f32[5,16,16]{2,1,0:T(8,128)}) custom-call(f32[16,1024]{1,0:T(8,128)S(1)} %get-tuple-element.6.left_i, f32[16,4096]{1,0:T(8,128)S(1)} %get-tuple-element.7.right_i, f32[5,16,16]{2,1,0:T(8,128)S(1)} %get-tuple-element.8.coef_i), custom_call_target="tpu_custom_call" | custom-call | tf_op jit(solution)/shard_map/pallas_call | solution.py:592
Async XLA Ops:
  1.3 0.7 copy-start
  1.9 0.7 copy-start.1
